TPU v7x, 32 devices: a whole 2x2x4 slice. The times are simulated.
32 devices in a mesh: depth: 4 (over y, core), tile: 8 (over z, x).
Axes of the slice: x: 2, y: 2, z: 4, core: 2. Of those that a mesh axis runs over, the one named last changes fastest.
Arguments:
- fields: float32 [2, 128, 128, 1024], P(None, 'depth', 'tile'), may hold values from -6 to 6
- colour_palette: float32 [3, 16], replicated, may hold values from 0.05 to 1
- opacity_palette: float32 [16], replicated, may hold values from 0.2 to 3
- tf_index: int32 [256], replicated, may hold values from 0 to 15
Outputs:
- image: float32 [4, 128, 1024], P(None, 'tile', 'depth')
All inputs are finite; a program needn't handle non-finite values.
Results may differ from a plain program's by a relative error of at most 0.0003.
Values sent between devices are 32-bit elements; how exact they have to be, the bound alone decides.
No kernel may reach another device: no remote copies, remote signals or barrier semaphores. Data moves between devices by JAX's collectives and lax.ppermute only.
A program may use at most 64 MiB of HBM per device.

v0:
```python
import functools

import jax
import jax.numpy as jnp
import ml_dtypes
import numpy as np
from jax import lax
from jax.experimental import pallas as pl
from jax.experimental.pallas import tpu as pltpu
from jax.sharding import Mesh
from jax.sharding import PartitionSpec as P


RAD = 4
LANES = 128
HALO = 8
GROUP = ("depth", "pair")
PER = LANES // (2 * RAD)

offsets = np.arange(-4.0, 5.0)
bell = np.exp(-(offsets**2) / 8.0)
S_TAPS = bell / np.sqrt(np.sum(bell**2))
slope_raw = offsets * bell
D_TAPS = slope_raw / np.sqrt(np.sum(slope_raw**2))


def split_np(matrix):
    hi = matrix.astype(ml_dtypes.bfloat16)
    lo = (matrix - hi.astype(np.float64)).astype(ml_dtypes.bfloat16)
    return hi, lo


def split(value):
    hi = value.astype(jnp.bfloat16)
    return hi, (value - hi.astype(jnp.float32)).astype(jnp.bfloat16)


def mxu(a, b):
    return jnp.dot(a, b, preferred_element_type=jnp.float32)


def band(taps, rows, cols, shift):
    matrix = np.zeros((rows, cols))
    for row in range(rows):
        for k in range(-RAD, RAD + 1):
            if 0 <= row + k + shift < cols:
                matrix[row, row + k + shift] = taps[k + RAD]
    return matrix


def symmetric(block, n):
    t = [float(x) for x in S_TAPS[RAD:]]
    out = t[0] * block[4 : 4 + n]
    for k in range(1, RAD + 1):
        out = out + t[k] * (block[4 - k : 4 - k + n] + block[4 + k : 4 + k + n])
    return out


def slope(block, n):
    t = [float(x) for x in D_TAPS[RAD:]]
    out = t[1] * (block[5 : 5 + n] - block[3 : 3 + n])
    for k in range(2, RAD + 1):
        out = out + t[k] * (block[4 + k : 4 + k + n] - block[4 - k : 4 - k + n])
    return out


def source_kernel(blocks, groups, which, edges, planes, *refs):
    fields_ref, bh_ref, bl_ref = refs[:3]
    outs, (held, us, in_sems, sems) = refs[3:-4], refs[-4:]
    if edges:
        flag_ref, outs = outs[-1], outs[:-1]
    joined = len(outs) == blocks
    slab, rows, columns = held.shape
    steps = slab // planes
    wide = 2 * LANES

    def fetch(step):
        part = pl.ds(step * planes, planes)
        return pltpu.make_async_copy(fields_ref.at[which, part], held.at[part], in_sems.at[step])

    for step in range(steps):
        fetch(step).start()

    def filtered(step):
        values = held[pl.ds(step * planes, planes)].reshape(planes * rows, columns)
        hi, lo = split(values)
        for j in range(columns // wide):
            left, right = max(0, wide * j - LANES), min(columns, wide * (j + 1) + LANES)
            base = left - (wide * j - LANES)
            bh = bh_ref[base : base + right - left]
            bl = bl_ref[base : base + right - left]
            u = mxu(hi[:, left:right], bh) + mxu(lo[:, left:right], bh) + mxu(hi[:, left:right], bl)
            for h in range(2):
                us[2 * j + h, pl.ds(step * planes, planes)] = u[
                    :, h * LANES : (h + 1) * LANES
                ].reshape(planes, rows, LANES)

    me = lax.axis_index(GROUP)
    place = lax.rem(me, groups)

    if edges:
        flag_ref[...] = jnp.zeros(flag_ref.shape, jnp.float32) + (place == groups - 1).astype(jnp.float32)

    def copies(at, first, count):
        found = []
        for m in range(blocks):
            for h in range(2):
                row = pl.multiple_of(HALO * (h ^ place), HALO)
                target = outs[m].at[h] if joined else outs[h * blocks + m]
                found.append(
                    pltpu.make_async_copy(
                        us.at[me ^ m, pl.ds(first, count), pl.ds(row, HALO)],
                        target.at[pl.ds(first, count)],
                        sems.at[at, 2 * m + h],
                    )
                )
        return found

    def collected(step):
        lane = lax.broadcasted_iota(jnp.int32, (rows, LANES), 1)
        zero = jnp.zeros((rows, LANES), jnp.float32)
        part = lax.rem(step, PER // planes) * planes
        at = slab + step * planes // PER
        for b in range(blocks):
            acc = us[b, at]
            for z in range(planes):
                before = us[b - 1, step * planes + z] if b > 0 else zero
                after = us[b + 1, step * planes + z] if b < blocks - 1 else zero
                both = jnp.where(lane >= LANES // 2, before, after)
                moved = pltpu.roll(both, lax.rem(RAD + 2 * RAD * (z + part), LANES), 1)
                acc = jnp.where(lane // (2 * RAD) == z + part, moved, acc)
            us[b, at] = acc

    def body(step, carry):
        fetch(step).wait()
        filtered(step)
        for copy in copies(step, step * planes, planes):
            copy.start()
        if edges:
            collected(step)
        return carry

    lax.fori_loop(0, steps, body, 0)
    last = copies(steps, slab, edges) if edges else []
    for copy in last:
        copy.start()
    for at in range(steps):
        for copy in copies(at, at * planes, planes):
            copy.wait()
    for copy in last:
        copy.wait()


def source(fields, which, groups, bh, bl, edges, joined, vmem):
    _, slab, rows, columns = fields.shape
    blocks = columns // LANES
    extra = slab // PER if edges else 0
    planes = 8
    steps = slab // planes
    block = (slab + extra, HALO, LANES)
    shapes = [(2,) + block] * blocks if joined else [block] * (2 * blocks)
    flag_spec = [pl.BlockSpec(memory_space=pltpu.VMEM)] if edges else []
    flag_shape = [(8, LANES)] if edges else []
    return pl.pallas_call(
        functools.partial(source_kernel, blocks, groups, which, extra, planes),
        in_specs=[pl.BlockSpec(memory_space=pltpu.HBM)] + [pl.BlockSpec(memory_space=pltpu.VMEM)] * 2,
        out_specs=[pl.BlockSpec(memory_space=pl.ANY)] * len(shapes) + flag_spec,
        out_shape=[jax.ShapeDtypeStruct(shape, jnp.float32) for shape in shapes + flag_shape],
        scratch_shapes=[
            pltpu.VMEM((slab, rows, columns), jnp.float32),
            pltpu.VMEM((blocks, slab + extra, rows, LANES), jnp.float32),
            pltpu.SemaphoreType.DMA((steps,)),
            pltpu.SemaphoreType.DMA((steps + 1, 2 * blocks)),
        ],
        compiler_params=pltpu.CompilerParams(vmem_limit_bytes=vmem),
        cost_estimate=cost(5),
        name="columns_filter",
    )(fields, bh, bl)


def cost(microseconds):
    return pl.CostEstimate(flops=0, bytes_accessed=int(microseconds * 3e6), transcendentals=0)


def gather_rows(groups, slab, extra, own, halos, zin, ein, sems):
    me = lax.axis_index(GROUP)
    first = HALO if halos else 0
    parts = []
    joined = len(own[0].shape) == 4
    blocks = len(own) if joined else len(own) // 2
    for m in range(blocks):
        d, g = (me ^ m) // groups, lax.rem(me ^ m, groups)
        for h in range(2):
            ref = own[m].at[h] if joined else own[h * blocks + m]
            parts.append((ref, d, first + HALO * (2 * g + (h ^ g))))
    end = zin.shape[1] - HALO
    leads = lax.rem(me, groups) == groups - 1
    narrow = halos and halos[0].shape[2] < HALO
    if halos and not narrow:
        for i in range(halos[0].shape[0]):
            d = (me // groups) ^ i
            parts.append((halos[0].at[i], d, jnp.where(leads, 0, end)))
            parts.append((halos[1].at[i], d, jnp.where(leads, end, 0)))
    copies = []
    for ref, d, row in parts:
        row = pl.multiple_of(row, HALO)
        copies.append(
            pltpu.make_async_copy(
                ref.at[pl.ds(0, slab)],
                zin.at[pl.ds(RAD + d * slab, slab), pl.ds(row, HALO)],
                sems.at[len(copies)],
            )
        )
        if extra:
            copies.append(
                pltpu.make_async_copy(
                    ref.at[pl.ds(slab, extra)],
                    ein.at[pl.ds(1 + d * extra, extra), pl.ds(row, HALO)],
                    sems.at[len(copies)],
                )
            )
    for copy in copies:
        copy.start()
    if narrow:
        for i in range(halos[0].shape[0]):
            part = pl.ds(RAD + ((me // groups) ^ i) * slab, slab)
            one, other = halos[0][i], halos[1][i]
            zin[part, HALO - RAD : HALO, :] = jnp.where(leads, one, other)
            zin[part, end : end + RAD, :] = jnp.where(leads, other, one)
    return copies


def clear_ends(ref, width):
    zero = jnp.zeros((width,) + ref.shape[1:], jnp.float32)
    ref[:width] = zero
    ref[ref.shape[0] - width :] = zero


def plane_smooth(zin, start, count):
    tiles = []
    for row in range(0, zin.shape[1], 8):
        tiles.append(symmetric(zin[pl.ds(start, count + 2 * RAD), row : row + 8, :], count))
    hi, lo = split(jnp.concatenate(tiles, axis=1))
    return jnp.concatenate([hi, lo, hi], axis=1)


def lookup(tables, index):
    return [jnp.take_along_axis(t, index, axis=1, mode="promise_in_bounds") for t in tables]


def first_kernel(groups, slab, extra, blocks, count_strips, factor, *refs):
    own, halos, refs = refs[: 2 * blocks], refs[2 * blocks : 2 * blocks + 2], refs[2 * blocks + 2 :]
    lhs_ref, yw_ref, zh_ref, zl_ref, pair_ref, pal_ref = refs[:6]
    outs = refs[6:-9]
    zin, ein, sm, gx, gy, es, found_ref, fraction_ref, sems = refs[-9:]
    copies = gather_rows(groups, slab, extra, own, halos, zin, ein, sems)
    planes = zin.shape[0] - 2 * RAD
    rows = sm.shape[1]
    wide = zin.shape[1]
    place = lax.axis_index("strips")
    case = (place == 0).astype(jnp.int32) + 2 * (place == count_strips - 1).astype(jnp.int32)
    lhs_ref = lhs_ref.at[case]
    clear_ends(zin, RAD)
    clear_ends(sm, RAD)
    clear_ends(ein, 1)
    for copy in copies:
        copy.wait()
    step = 8

    near = [ein[j] for j in range(ein.shape[0])]
    count = len(near) - 2
    stacked = jnp.concatenate(
        [jnp.concatenate(near[k : k + count], axis=0) for k in range(3)], axis=1
    )
    hi, lo = split(stacked)
    ez = mxu(hi, zh_ref[...]) + mxu(lo, zh_ref[...]) + mxu(hi, zl_ref[...])
    hi, lo = split(ez.reshape(count, wide, LANES))
    stack = jnp.concatenate([hi, lo, hi], axis=1)
    for j in range(0, count, 2):
        out = mxu(lhs_ref[:rows], jnp.concatenate([stack[j], stack[j + 1]], axis=1))
        es[j] = out[:, :LANES]
        es[j + 1] = out[:, LANES:]

    def smooth_stage(t):
        start = pl.multiple_of(t * step, step)
        stack = plane_smooth(zin, start, step)
        for q in range(0, step, 2):
            out = mxu(lhs_ref[...], jnp.concatenate([stack[q], stack[q + 1]], axis=1))
            for h in range(2):
                part = out[:, h * LANES : (h + 1) * LANES]
                sm[RAD + start + q + h] = part[:rows]
                gx[start + q + h] = part[rows:]

    def across_stage(t):
        start = pl.multiple_of(t * step, step)
        group = es[start // PER]
        moved = []
        for i in range(step):
            shift = (LANES - 2 * RAD * (lax.rem(start, PER) + i)) % LANES
            moved.append(pltpu.roll(group, shift, 1))
        moved = jnp.concatenate(moved, axis=0)
        own_rows = sm[pl.ds(RAD + start, step)].reshape(step * rows, LANES)
        hi, lo = split(jnp.concatenate([own_rows, moved], axis=1))
        out = mxu(hi, yw_ref[...])
        out = out[:, :LANES] + out[:, LANES:] + mxu(lo, yw_ref[:, :LANES])
        gy[pl.ds(start, step)] = out.reshape(step, rows, LANES)

    halves = pair_ref.shape[0]
    bins = halves * LANES
    half = 0.5 * (bins - 1)

    def index_stage(t):
        start = pl.multiple_of(t * step, step)
        pairs = [jnp.broadcast_to(pair_ref[h], (8, LANES)) for h in range(halves)]
        for row in range(0, rows, 8):
            level = half * jnp.tanh(0.75 * sm[pl.ds(RAD + start, step), row : row + 8, :]) + half
            index = jnp.minimum(level.astype(jnp.int32), bins - 2)
            fraction_ref[t & 1, :, row : row + 8, :] = level - index.astype(jnp.float32)
            at = index & (LANES - 1)
            found = [lookup(pairs, at[i]) for i in range(step)]
            for i in range(step):
                pair = found[i][0]
                for h in range(1, halves):
                    pair = jnp.where(index[i] >= h * LANES, found[i][h], pair)
                found_ref[t & 1, i, row : row + 8, :] = pair

    def colour_stage(t):
        start = pl.multiple_of(t * step, step)
        colours = [jnp.broadcast_to(pal_ref[c], (8, LANES)) for c in range(4)]
        for row in range(0, rows, 8):
            if row == 0 or row == rows - 8:
                o_ref, at = outs[0], min(row, 8)
            else:
                o_ref, at = outs[1], row - 8
            pair = found_ref[t & 1, :, row : row + 8, :]
            fraction = fraction_ref[t & 1, :, row : row + 8, :]
            low, high = pair & (LANES - 1), pair >> 7
            first = [lookup(colours, low[i]) for i in range(step)]
            second = [lookup(colours, high[i]) for i in range(step)]
            grad_z = slope(sm[pl.ds(start, step + 2 * RAD), row : row + 8, :], step)
            grad_x = gx[pl.ds(start, step), row : row + 8, :]
            grad_y = gy[pl.ds(start, step), row : row + 8, :]
            facing = jnp.abs(0.26726 * grad_z + 0.53452 * grad_x + 0.80178 * grad_y)
            square = jnp.maximum(grad_z * grad_z + grad_x * grad_x + grad_y * grad_y, 0.1)
            shade = 0.3 + 0.7 * facing * lax.rsqrt(square)
            for i in range(step):
                for c in range(4):
                    looked = first[i][c] + fraction[i] * (second[i][c] - first[i][c])
                    o_ref[c, start + i, at : at + 8, :] = looked * (shade[i] if c < 3 else factor)

    steps = planes // step
    smooth_stage(0)
    index_stage(0)
    across_stage(0)
    smooth_stage(1)

    def body(t, carry):
        colour_stage(t - 2)
        index_stage(t - 1)
        across_stage(t - 1)
        smooth_stage(t)
        return carry

    lax.fori_loop(2, steps, body, 0)
    colour_stage(steps - 2)
    index_stage(steps - 1)
    across_stage(steps - 1)
    colour_stage(steps - 1)


def second_kernel(groups, slab, blocks, haloed, joins, *refs):
    own, refs = refs[:blocks], refs[blocks:]
    halos, refs = (refs[:2], refs[2:]) if haloed else ((), refs)
    (lhs_ref, c_ref), (zin, sm, sems) = refs[:2], refs[-3:]
    image_ref, outs = (refs[2], refs[3:-3]) if joins else (None, refs[2:-3])
    copies = gather_rows(groups, slab, 0, own, halos, zin, None, sems)
    planes = zin.shape[0] - 2 * RAD
    rows = sm.shape[1]
    step = 8

    clear_ends(zin, RAD)
    for copy in copies:
        copy.wait()

    def march(t, carry):
        start = pl.multiple_of(t * step, step)
        stack = plane_smooth(zin, start, step)
        for q in range(0, step, 2):
            out = mxu(lhs_ref[...], jnp.concatenate([stack[q], stack[q + 1]], axis=1))
            sm[q] = out[:, :LANES]
            sm[q + 1] = out[:, LANES:]
        through, red, green, blue = carry
        for i in range(step):
            sigmoid = 0.5 * jnp.tanh(sm[i]) + 0.5
            passed = through * jnp.exp(-(c_ref[3, start + i] * sigmoid))
            weight = through - passed
            red = red + weight * c_ref[0, start + i]
            green = green + weight * c_ref[1, start + i]
            blue = blue + weight * c_ref[2, start + i]
            through = passed
        return through, red, green, blue

    zero = jnp.zeros((rows, LANES), jnp.float32)
    through, red, green, blue = lax.fori_loop(
        0, planes // step, march, (zero + 1.0, zero, zero, zero)
    )
    first = lax.rem(lax.axis_index(GROUP), groups) == 0
    for c, value in enumerate((red, green, blue, through)):
        if joins:
            strips = (
                jnp.concatenate([value[:8], image_ref[c, :8]], axis=0),
                jnp.concatenate([image_ref[c, 8:], value[8:]], axis=0),
            )
            outs[0][c] = jnp.where(first, strips[0], strips[1])
            outs[1][c] = jnp.where(first, strips[1], strips[0])
        else:
            outs[0][c] = value


def vmem_call(kernel, shapes, scratch, in_specs, microseconds, limit):
    return pl.pallas_call(
        kernel,
        in_specs=in_specs,
        out_specs=[pl.BlockSpec(memory_space=pltpu.VMEM)] * len(shapes),
        out_shape=[jax.ShapeDtypeStruct(shape, jnp.float32) for shape in shapes],
        scratch_shapes=scratch,
        compiler_params=pltpu.CompilerParams(vmem_limit_bytes=limit << 20),
        cost_estimate=cost(microseconds),
    )


def exchange(blocks, order):
    blocks = list(blocks)
    got = blocks[:1] + [None] * (len(blocks) - 1)
    for m in order:
        pairs = [(s, s ^ m) for s in range(len(blocks))]
        got[m] = lax.ppermute(blocks[m], GROUP, pairs)
    return got


def row_halo(blocks, groups, count, leads):
    joined = blocks[0].ndim == 4
    total = len(blocks) if joined else len(blocks) // 2
    found = []
    for which in range(2):
        half, member = (0, which) if groups > 1 else (1 - which, 0)
        edge = []
        for i in range(total // groups):
            m = groups * i + member
            if joined:
                low, high = blocks[m][half, :, :RAD], blocks[m][half, :, HALO - RAD :]
                edge.append(jnp.where(leads, low, high) if which else jnp.where(leads, high, low))
            else:
                edge.append(blocks[half * total + m])
        pairs = []
        for strip in range(count):
            for g in range(groups):
                other = strip + (1 if (g == groups - 1) == (which == 0) else -1)
                if 0 <= other < count:
                    pairs.append((strip * groups + g, other * groups + g))
        found.append(lax.ppermute(jnp.stack(edge), ("strips", "pair"), pairs))
    return found


def three_terms(matrix):
    hi, lo = split_np(matrix)
    return np.concatenate([hi, hi, lo], axis=1)


def local(depth, count, groups, fields, colour_palette, opacity_palette, tf_index):
    slab, strip, _ = fields.shape[1:]
    extra = slab // PER
    planes = slab * depth
    rows = strip * groups
    wide = rows + 2 * HALO
    bins = tf_index.shape[0]
    blocks = depth * groups

    bh, bl = split_np(band(S_TAPS, 2 * LANES, 4 * LANES, LANES).T)
    smooth_rows = band(S_TAPS, rows + 2 * RAD, wide, HALO - RAD)
    slope_rows = band(D_TAPS, rows, rows + 2 * RAD, RAD)
    inner = slice(HALO, rows - HALO)
    outer = np.r_[0:HALO, rows - HALO : rows]
    forms = []
    for case in range(4):
        inside = np.ones((rows + 2 * RAD, 1))
        if case & 1:
            inside[:RAD] = 0
        if case & 2:
            inside[-RAD:] = 0
        smooth, gradient = smooth_rows[RAD:-RAD], slope_rows @ (inside * smooth_rows)
        forms.append(three_terms(np.concatenate([smooth, gradient], axis=0)))
    edge_form = three_terms(smooth[outer])
    inner_form = three_terms(smooth[inner][:, HALO:-HALO])
    form = jnp.asarray(np.stack(forms))
    across = np.zeros((2 * LANES, LANES))
    across[:LANES] = band(D_TAPS, LANES, LANES, 0).T
    for lane in range(LANES):
        for k in range(-RAD, RAD + 1):
            if lane + k < 0:
                across[LANES + lane + k + RAD, lane] = D_TAPS[k + RAD]
            if lane + k >= LANES:
                across[LANES + RAD + lane + k - LANES, lane] = D_TAPS[k + RAD]
    yw = np.concatenate(split_np(across), axis=1)
    zh, zl = split_np(np.kron(band(S_TAPS, PER, 3 * PER, PER).T, np.eye(2 * RAD)))

    following = jnp.concatenate([tf_index[1:], tf_index[-1:]])
    pair = (tf_index + LANES * following).reshape(bins // LANES, 1, LANES)
    palette = jnp.concatenate([colour_palette, opacity_palette[None]], axis=0)
    palette = jnp.pad(palette, ((0, 0), (0, LANES - palette.shape[1])))[:, None, :]

    anywhere = pl.BlockSpec(memory_space=pl.ANY)
    vmem = pl.BlockSpec(memory_space=pltpu.VMEM)
    f32 = jnp.float32

    def colours(own, halos, lhs):
        shapes = [(4, planes, len(outer), LANES)]
        if rows > len(outer):
            shapes.append((4, planes, rows - len(outer), LANES))
        return vmem_call(
            functools.partial(first_kernel, groups, slab, extra, blocks, count, 1.5 * (2.0 / planes)),
            shapes,
            [
                pltpu.VMEM((planes + 2 * RAD, wide, LANES), f32),
                pltpu.VMEM((planes // PER + 2, wide, LANES), f32),
                pltpu.VMEM((planes + 2 * RAD, rows, LANES), f32),
                pltpu.VMEM((planes, rows, LANES), f32),
                pltpu.VMEM((planes, rows, LANES), f32),
                pltpu.VMEM((planes // PER, rows, LANES), f32),
                pltpu.VMEM((2, 8, rows, LANES), jnp.int32),
                pltpu.VMEM((2, 8, rows, LANES), f32),
                pltpu.SemaphoreType.DMA((4 * (blocks + depth),)),
            ],
            [anywhere] * (2 * blocks + 2) + [vmem] * 6,
            20,
            16,
        )(*own, *halos, lhs, yw, zh, zl, pair, palette)

    def march(own, halos, lhs, coloured, *others):
        mine, out = (wide, len(outer)) if halos else (rows, rows - len(outer))
        return vmem_call(
            functools.partial(second_kernel, groups, slab, blocks, bool(halos), bool(others)),
            [(4, out, LANES)] * (1 + len(others)),
            [
                pltpu.VMEM((planes + 2 * RAD, mine, LANES), f32),
                pltpu.VMEM((8, out, LANES), f32),
                pltpu.SemaphoreType.DMA((2 * blocks,)),
            ],
            [anywhere] * blocks + [vmem] * (len(halos) + 2 + len(others)),
            5,
            10,
        )(*own, *halos, lhs, coloured, *others)

    order = sorted(range(1, blocks), key=lambda m: (bin(m).count("1"), m))
    sent0 = list(source(fields, 0, groups, bh, bl, True, False, 60 << 20))
    leads = sent0.pop()[0] > 0.5
    got0 = exchange(sent0[:blocks], order) + exchange(sent0[blocks:], order)
    bh, pair, palette = lax.optimization_barrier((jnp.asarray(bh), pair, palette))
    sent1 = source(fields, 1, groups, bh, bl, False, True, 16 << 20)
    halo0 = row_halo(got0, groups, count, leads)
    got1 = exchange(sent1, order)
    halo1 = row_halo(got1, groups, count, leads)
    coloured = colours(got0, halo0, form)
    others = ()
    if rows > len(outer):
        others = march(got1, (), inner_form, coloured[1])
    image = march(got1, halo1, edge_form, coloured[0], *others)
    if groups == 1:
        return image[0]
    given = lax.ppermute(image[1], "pair", [(0, 1), (1, 0)])
    return jnp.concatenate(
        [jnp.where(leads, given, image[0]), jnp.where(leads, image[0], given)], axis=2
    )


def solution(mesh):
    depth, tiles = mesh.devices.shape

    def program(fields, colour_palette, opacity_palette, tf_index):
        groups = max(1, fields.shape[3] // (LANES * depth))
        count = tiles // groups
        finer = Mesh(mesh.devices.reshape(depth, count, groups), ("depth", "strips", "pair"))

        def body(*arrays):
            return local(depth, count, groups, *arrays)

        mapped = jax.shard_map(
            body,
            mesh=finer,
            in_specs=(P(None, "depth", ("strips", "pair"), None), P(), P(), P()),
            out_specs=P(None, ("strips", "pair"), "depth"),
            check_vma=False,
        )
        return mapped(fields, colour_palette, opacity_palette, tf_index)

    return program
```

profile of v0, /device:TPU:0, one launch (start us, length us, event | category | flops | bytes accessed | tf_op | source)
XLA Modules:
  0.0 110.2 jit_solution(5538566999035396855)
XLA Ops:
  0.0 9.0 %columns_filter.2 = (f32[34,8,128]{2,1,0:T(8,128)}, f32[34,8,128]{2,1,0:T(8,128)}, f32[34,8,128]{2,1,0:T(8,128)}, f32[34,8,128]{2,1,0:T(8,128)}, f32[34,8,128]{2...) custom-call(f32[2,32,16,1024]{3,2,1,0:T(8,128)} %refs_0_.3, ...), custom_call_target="tpu_custom_call" | custom-call | bytes 15000000 | tf_op jit(solution)/shard_map/columns_filter/pallas_call | solution.py:164
  9.0 4.0 %collective-permute-start.13 = (f32[34,8,128]{2,1,0:T(8,128)}, f32[34,8,128]{2,1,0:T(8,128)S(1)}, u32[]{:S(2)}, u32[]{:S(2)}) collective-permute-start(f32[34,8,128]{2,1,0:T(8,128)} %get-tuple-element.52), channel_id=1, source_target_pairs={{0,17},{1,16},{8,25},{9,24},{16,1},{17,0},{24,9},{25,8},{2,19},{3,... | collective-permute-start | bytes 417800 | tf_op jit(solution)/shard_map/ppermute | solution.py:437
  13.0 1.1 %collective-permute-start.9 = (f32[34,8,128]{2,1,0:T(8,128)}, f32[34,8,128]{2,1,0:T(8,128)S(1)}, u32[]{:S(2)}, u32[]{:S(2)}) collective-permute-start(f32[34,8,128]{2,1,0:T(8,128)} %get-tuple-element.48), channel_id=1, source_target_pairs={{0,1},{1,0},{8,9},{9,8},{16,17},{17,16},{24,25},{25,24},{2,3},{3,2... | collective-permute-start | bytes 417800 | tf_op jit(solution)/shard_map/ppermute | solution.py:437
  15.3 0.6 fusion
  16.0 2.2 %copy-done = f32[2,32,16,1024]{3,2,1,0:T(8,128)S(1)} copy-done((f32[2,32,16,1024]{3,2,1,0:T(8,128)S(1)}, f32[2,32,16,1024]{3,2,1,0:T(8,128)}, u32[]{:S(2)}) %copy-start) | copy-done | bytes 4194328
  18.4 3.8 %columns_filter.3 = (f32[2,32,8,128]{3,2,1,0:T(8,128)S(1)}, f32[2,32,8,128]{3,2,1,0:T(8,128)S(1)}, f32[2,32,8,128]{3,2,1,0:T(8,128)S(1)}, f32[2,32,8,128]{3,2,1,...) custom-call(f32[2,32,16,1024]{3,2,1,0:T(8,128)S(1)} %copy-done, ...), custom_call_target="tpu_custom_call" | custom-call | bytes 15000000 | tf_op jit(solution)/shard_map/columns_filter/pallas_call | solution.py:164
  22.1 1.8 %collective-permute-start = (f32[2,32,8,128]{3,2,1,0:T(8,128)S(1)}, f32[2,32,8,128]{3,2,1,0:T(8,128)S(1)}, u32[]{:S(2)}, u32[]{:S(2)}) collective-permute-start(f32[2,32,8,128]{3,2,1,0:T(8,128)S(1)} %get-tuple-element.40), channel_id=1, source_target_pairs={{0,1},{1,0},{8,9},{9,8},{16,17},{17,16},{24,25},{25,24},{2,3},{3,2... | collective-permute-start | bytes 786440 | tf_op jit(solution)/shard_map/ppermute | solution.py:437
  24.5 1.5 %collective-permute-start.12 = (f32[34,8,128]{2,1,0:T(8,128)S(1)}, f32[34,8,128]{2,1,0:T(8,128)S(1)}, u32[]{:S(2)}, u32[]{:S(2)}) collective-permute-start(f32[34,8,128]{2,1,0:T(8,128)S(1)} %copy-done.22), channel_id=1, source_target_pairs={{0,16},{1,17},{8,24},{9,25},{16,0},{17,1},{24,8},{25,9},{2,18},{3,... | collective-permute-start | bytes 417800 | tf_op jit(solution)/shard_map/ppermute | solution.py:437
  26.3 1.9 %collective-permute-start.2 = (f32[2,32,8,128]{3,2,1,0:T(8,128)S(1)}, f32[2,32,8,128]{3,2,1,0:T(8,128)S(1)}, u32[]{:S(2)}, u32[]{:S(2)}) collective-permute-start(f32[2,32,8,128]{3,2,1,0:T(8,128)S(1)} %get-tuple-element.42), channel_id=1, source_target_pairs={{0,9},{1,8},{8,1},{9,0},{16,25},{17,24},{24,17},{25,16},{2,11},{3,... | collective-permute-start | bytes 786440 | tf_op jit(solution)/shard_map/ppermute | solution.py:437
  28.2 2.7 %collective-permute-done.12.refs_4_ = f32[34,8,128]{2,1,0:T(8,128)S(1)} collective-permute-done((f32[34,8,128]{2,1,0:T(8,128)S(1)}, f32[34,8,128]{2,1,0:T(8,128)S(1)}, u32[]{:S(2)}, u32[]{:S(2)}) %collective-permute-start.12) | collective-permute-done | bytes 139296 | tf_op jit(solution)/shard_map/ppermute | solution.py:437
  30.9 1.6 %collective-permute-start.3 = (f32[2,32,8,128]{3,2,1,0:T(8,128)S(1)}, f32[2,32,8,128]{3,2,1,0:T(8,128)S(1)}, u32[]{:S(2)}, u32[]{:S(2)}) collective-permute-start(f32[2,32,8,128]{3,2,1,0:T(8,128)S(1)} %get-tuple-element.43), channel_id=1, source_target_pairs={{0,16},{1,17},{8,24},{9,25},{16,0},{17,1},{24,8},{25,9},{2,18},{3,... | collective-permute-start | bytes 786440 | tf_op jit(solution)/shard_map/ppermute | solution.py:437
  33.0 0.9 collective-permute-start.4
  33.9 1.9 %collective-permute-start.5 = (f32[2,32,8,128]{3,2,1,0:T(8,128)S(1)}, f32[2,32,8,128]{3,2,1,0:T(8,128)S(1)}, u32[]{:S(2)}, u32[]{:S(2)}) collective-permute-start(f32[2,32,8,128]{3,2,1,0:T(8,128)S(1)} %get-tuple-element.45), channel_id=1, source_target_pairs={{0,24},{1,25},{8,16},{9,17},{16,8},{17,9},{24,0},{25,1},{2,26},{3,... | collective-permute-start | bytes 786440 | tf_op jit(solution)/shard_map/ppermute | solution.py:437
  36.4 0.7 compare_bitcast_fusion
  37.2 1.1 collective-permute-start.16
  38.3 13.1 %collective-permute-done.3.refs_4_ = f32[2,32,8,128]{3,2,1,0:T(8,128)S(1)} collective-permute-done((f32[2,32,8,128]{3,2,1,0:T(8,128)S(1)}, f32[2,32,8,128]{3,2,1,0:T(8,128)S(1)}, u32[]{:S(2)}, u32[]{:S(2)}) %collective-permute-start.3) | collective-permute-done | bytes 262176 | tf_op jit(solution)/shard_map/ppermute | solution.py:437
  51.9 2.7 %collective-permute-done.5.refs_6_ = f32[2,32,8,128]{3,2,1,0:T(8,128)S(1)} collective-permute-done((f32[2,32,8,128]{3,2,1,0:T(8,128)S(1)}, f32[2,32,8,128]{3,2,1,0:T(8,128)S(1)}, u32[]{:S(2)}, u32[]{:S(2)}) %collective-permute-start.5) | collective-permute-done | bytes 262176 | tf_op jit(solution)/shard_map/ppermute | solution.py:437
  54.6 3.5 %collective-permute-start.24 = (f32[4,34,8,128]{3,2,1,0:T(8,128)S(1)}, f32[4,34,8,128]{3,2,1,0:T(8,128)S(1)}, u32[]{:S(2)}, u32[]{:S(2)}) collective-permute-start(f32[4,34,8,128]{3,2,1,0:T(8,128)S(1)} %pad_maximum_fusion.1), channel_id=1, source_target_pairs={{0,2},{2,4},{3,1},{4,6},{5,3},{7,5},{8,10},{10,12},{11,9},{12,14},... | collective-permute-start | bytes 1671176 | tf_op jit(solution)/shard_map/ppermute | solution.py:461
  58.1 1.3 %collective-permute-start.23 = (f32[4,34,8,128]{3,2,1,0:T(8,128)S(1)}, f32[4,34,8,128]{3,2,1,0:T(8,128)S(1)}, u32[]{:S(2)}, u32[]{:S(2)}) collective-permute-start(f32[4,34,8,128]{3,2,1,0:T(8,128)S(1)} %pad_maximum_fusion), channel_id=1, source_target_pairs={{1,3},{2,0},{3,5},{4,2},{5,7},{6,4},{9,11},{10,8},{11,13},{12,10},... | collective-permute-start | bytes 1671176 | tf_op jit(solution)/shard_map/ppermute | solution.py:461
  59.6 1.1 collective-permute-start.19
  60.7 2.0 %collective-permute-start.20 = (f32[34,8,128]{2,1,0:T(8,128)S(1)}, f32[34,8,128]{2,1,0:T(8,128)S(1)}, u32[]{:S(2)}, u32[]{:S(2)}) collective-permute-start(f32[34,8,128]{2,1,0:T(8,128)S(1)} %copy-done.16), channel_id=1, source_target_pairs={{0,17},{1,16},{8,25},{9,24},{16,1},{17,0},{24,9},{25,8},{2,19},{3,... | collective-permute-start | bytes 417800 | tf_op jit(solution)/shard_map/ppermute | solution.py:437
  62.8 1.1 %collective-permute-start.21 = (f32[34,8,128]{2,1,0:T(8,128)S(1)}, f32[34,8,128]{2,1,0:T(8,128)S(1)}, u32[]{:S(2)}, u32[]{:S(2)}) collective-permute-start(f32[34,8,128]{2,1,0:T(8,128)S(1)} %copy-done.15), channel_id=1, source_target_pairs={{0,24},{1,25},{8,16},{9,17},{16,8},{17,9},{24,0},{25,1},{2,26},{3,... | collective-permute-start | bytes 417800 | tf_op jit(solution)/shard_map/ppermute | solution.py:437
  64.0 5.2 %collective-permute-done.19.refs_12_ = f32[34,8,128]{2,1,0:T(8,128)S(1)} collective-permute-done((f32[34,8,128]{2,1,0:T(8,128)S(1)}, f32[34,8,128]{2,1,0:T(8,128)S(1)}, u32[]{:S(2)}, u32[]{:S(2)}) %collective-permute-start.19) | collective-permute-done | bytes 139296 | tf_op jit(solution)/shard_map/ppermute | solution.py:437
  69.2 4.6 %collective-permute-start.8 = (f32[4,32,4,128]{3,2,1,0:T(4,128)S(1)}, f32[4,32,4,128]{3,2,1,0:T(4,128)S(1)}, u32[]{:S(2)}, u32[]{:S(2)}) collective-permute-start(f32[4,32,4,128]{3,2,1,0:T(4,128)S(1)} %pad_maximum_fusion.3), channel_id=1, source_target_pairs={{0,2},{2,4},{3,1},{4,6},{5,3},{7,5},{8,10},{10,12},{11,9},{12,14},... | collective-permute-start | bytes 786440 | tf_op jit(solution)/shard_map/ppermute | solution.py:461
  73.8 1.3 %collective-permute-start.7 = (f32[4,32,4,128]{3,2,1,0:T(4,128)S(1)}, f32[4,32,4,128]{3,2,1,0:T(4,128)S(1)}, u32[]{:S(2)}, u32[]{:S(2)}) collective-permute-start(f32[4,32,4,128]{3,2,1,0:T(4,128)S(1)} %pad_maximum_fusion.2), channel_id=1, source_target_pairs={{1,3},{2,0},{3,5},{4,2},{5,7},{6,4},{9,11},{10,8},{11,13},{12,10},... | collective-permute-start | bytes 786440 | tf_op jit(solution)/shard_map/ppermute | solution.py:461
  75.1 1.1 collective-permute-start.22
  76.2 5.8 %collective-permute-done.22.refs_15_ = f32[34,8,128]{2,1,0:T(8,128)S(1)} collective-permute-done((f32[34,8,128]{2,1,0:T(8,128)S(1)}, f32[34,8,128]{2,1,0:T(8,128)S(1)}, u32[]{:S(2)}, u32[]{:S(2)}) %collective-permute-start.22) | collective-permute-done | bytes 139296 | tf_op jit(solution)/shard_map/ppermute | solution.py:437
  82.1 14.7 %shard_map.118 = (f32[4,128,16,128]{3,2,1,0:T(8,128)S(1)}, f32[4,128,16,128]{3,2,1,0:T(8,128)S(1)}) custom-call(f32[34,8,128]{2,1,0:T(8,128)S(1)} %copy-done.3, f32[34,8,128]{2,1,0:T(8,128)S(1)} %collective-permute-done.9.refs_1_, f32[34,8,128]{2,1,0:T(8,128)S(1)} %collective-permute-done.10.refs_2_, f32[34,8,128]{2,1,0:T(8,128)S(1)} %collective-permute-done.11.refs_3_, ...), custom_call_target="tpu_custom_call" | custom-call | bytes 60000000 | tf_op jit(solution)/shard_map/pallas_call | solution.py:520
  96.8 4.0 %shard_map.119.refs_12_ = f32[4,16,128]{2,1,0:T(8,128)S(1)} custom-call(f32[2,32,8,128]{3,2,1,0:T(8,128)S(1)} %get-tuple-element.39.refs_0_, f32[2,32,8,128]{3,2,1,0:T(8,128)S(1)} %collective-permute-done.refs_1_, f32[2,32,8,128]{3,2,1,0:T(8,128)S(1)} %collective-permute-done.1.refs_2_, f32[2,32,8,128]{3,2,1,0:T(8,128)S(1)} %collective-permute-done.2.refs_3_, ...), custom_call_target="tpu_custom_call" | custom-call | bytes 15000000 | tf_op jit(solution)/shard_map/pallas_call | solution.py:541
  100.9 4.6 %shard_map.120 = (f32[4,16,128]{2,1,0:T(8,128)S(1)}, f32[4,16,128]{2,1,0:T(8,128)S(1)}) custom-call(f32[2,32,8,128]{3,2,1,0:T(8,128)S(1)} %get-tuple-element.39.refs_0_, f32[2,32,8,128]{3,2,1,0:T(8,128)S(1)} %collective-permute-done.refs_1_, f32[2,32,8,128]{3,2,1,0:T(8,128)S(1)} %collective-permute-done.1.refs_2_, ...), custom_call_target="tpu_custom_call" | custom-call | bytes 15000000 | tf_op jit(solution)/shard_map/pallas_call | solution.py:541
  105.6 0.7 collective-permute-start.25
  106.3 3.3 %collective-permute-done.25 = f32[4,16,128]{2,1,0:T(8,128)S(1)} collective-permute-done((f32[4,16,128]{2,1,0:T(8,128)S(1)}, f32[4,16,128]{2,1,0:T(8,128)S(1)}, u32[]{:S(2)}, u32[]{:S(2)}) %collective-permute-start.25) | collective-permute-done | bytes 32800 | tf_op jit(solution)/shard_map/ppermute | solution.py:570
  (85 shorter events, 4.8 us)
Async XLA Ops:
  9.0 15.0 %collective-permute-start.13 = (f32[34,8,128]{2,1,0:T(8,128)}, f32[34,8,128]{2,1,0:T(8,128)S(1)}, u32[]{:S(2)}, u32[]{:S(2)}) collective-permute-start(f32[34,8,128]{2,1,0:T(8,128)} %get-tuple-element.52), channel_id=1, source_target_pairs={{0,17},{1,16},{8,25},{9,24},{16,1},{17,0},{24,9},{25,8},{2,19},{3,... | collective-permute-start | bytes 417800 | tf_op jit(solution)/shard_map/ppermute | solution.py:437
  13.0 11.0 %collective-permute-start.15 = (f32[34,8,128]{2,1,0:T(8,128)}, f32[34,8,128]{2,1,0:T(8,128)S(1)}, u32[]{:S(2)}, u32[]{:S(2)}) collective-permute-start(f32[34,8,128]{2,1,0:T(8,128)} %get-tuple-element.54), channel_id=1, source_target_pairs={{0,25},{1,24},{8,17},{9,16},{16,9},{17,8},{24,1},{25,0},{2,27},{3,... | collective-permute-start | bytes 417800 | tf_op jit(solution)/shard_map/ppermute | solution.py:437
  13.0 11.5 %collective-permute-start.9 = (f32[34,8,128]{2,1,0:T(8,128)}, f32[34,8,128]{2,1,0:T(8,128)S(1)}, u32[]{:S(2)}, u32[]{:S(2)}) collective-permute-start(f32[34,8,128]{2,1,0:T(8,128)} %get-tuple-element.48), channel_id=1, source_target_pairs={{0,1},{1,0},{8,9},{9,8},{16,17},{17,16},{24,25},{25,24},{2,3},{3,2... | collective-permute-start | bytes 417800 | tf_op jit(solution)/shard_map/ppermute | solution.py:437
  14.1 12.2 %collective-permute-start.11 = (f32[34,8,128]{2,1,0:T(8,128)}, f32[34,8,128]{2,1,0:T(8,128)S(1)}, u32[]{:S(2)}, u32[]{:S(2)}) collective-permute-start(f32[34,8,128]{2,1,0:T(8,128)} %get-tuple-element.50), channel_id=1, source_target_pairs={{0,9},{1,8},{8,1},{9,0},{16,25},{17,24},{24,17},{25,16},{2,11},{3,... | collective-permute-start | bytes 417800 | tf_op jit(solution)/shard_map/ppermute | solution.py:437
  18.3 63.7 %copy-start.4 = (f32[34,8,128]{2,1,0:T(8,128)S(1)}, f32[34,8,128]{2,1,0:T(8,128)}, u32[]{:S(2)}) copy-start(f32[34,8,128]{2,1,0:T(8,128)} %get-tuple-element.55.refs_8_) | copy-start | bytes 417796
  18.3 63.7 %copy-start.5 = (bf16[4,64,144]{2,1,0:T(8,128)(2,1)S(1)}, bf16[4,64,144]{2,1,0:T(8,128)(2,1)}, u32[]{:S(2)}) copy-start(bf16[4,64,144]{2,1,0:T(8,128)(2,1)} %constant.23.clone.refs_18_) | copy-start | bytes 221188
  18.3 63.7 %copy-start.6 = (bf16[256,256]{1,0:T(8,128)(2,1)S(1)}, bf16[256,256]{1,0:T(8,128)(2,1)}, u32[]{:S(2)}) copy-start(bf16[256,256]{1,0:T(8,128)(2,1)} %constant.26.clone.refs_19_) | copy-start | bytes 393220
  18.3 63.7 %copy-start.7 = (bf16[384,128]{1,0:T(8,128)(2,1)S(1)}, bf16[384,128]{1,0:T(8,128)(2,1)}, u32[]{:S(2)}) copy-start(bf16[384,128]{1,0:T(8,128)(2,1)} %constant.27.clone.refs_20_) | copy-start | bytes 294916
  18.3 63.7 %copy-start.8 = (bf16[384,128]{1,0:T(8,128)(2,1)S(1)}, bf16[384,128]{1,0:T(8,128)(2,1)}, u32[]{:S(2)}) copy-start(bf16[384,128]{1,0:T(8,128)(2,1)} %constant.28.clone.refs_21_) | copy-start | bytes 294916
  22.1 11.8 %collective-permute-start = (f32[2,32,8,128]{3,2,1,0:T(8,128)S(1)}, f32[2,32,8,128]{3,2,1,0:T(8,128)S(1)}, u32[]{:S(2)}, u32[]{:S(2)}) collective-permute-start(f32[2,32,8,128]{3,2,1,0:T(8,128)S(1)} %get-tuple-element.40), channel_id=1, source_target_pairs={{0,1},{1,0},{8,9},{9,8},{16,17},{17,16},{24,25},{25,24},{2,3},{3,2... | collective-permute-start | bytes 786440 | tf_op jit(solution)/shard_map/ppermute | solution.py:437
  23.9 11.9 %collective-permute-start.1 = (f32[2,32,8,128]{3,2,1,0:T(8,128)S(1)}, f32[2,32,8,128]{3,2,1,0:T(8,128)S(1)}, u32[]{:S(2)}, u32[]{:S(2)}) collective-permute-start(f32[2,32,8,128]{3,2,1,0:T(8,128)S(1)} %get-tuple-element.41), channel_id=1, source_target_pairs={{0,8},{1,9},{8,0},{9,1},{16,24},{17,25},{24,16},{25,17},{2,10},{3,... | collective-permute-start | bytes 786440 | tf_op jit(solution)/shard_map/ppermute | solution.py:437
  24.0 2.4 %collective-permute-start.10 = (f32[34,8,128]{2,1,0:T(8,128)S(1)}, f32[34,8,128]{2,1,0:T(8,128)S(1)}, u32[]{:S(2)}, u32[]{:S(2)}) collective-permute-start(f32[34,8,128]{2,1,0:T(8,128)S(1)} %copy-done.23), channel_id=1, source_target_pairs={{0,8},{1,9},{8,0},{9,1},{16,24},{17,25},{24,16},{25,17},{2,10},{3,... | collective-permute-start | bytes 417800 | tf_op jit(solution)/shard_map/ppermute | solution.py:437
  24.5 6.5 %collective-permute-start.12 = (f32[34,8,128]{2,1,0:T(8,128)S(1)}, f32[34,8,128]{2,1,0:T(8,128)S(1)}, u32[]{:S(2)}, u32[]{:S(2)}) collective-permute-start(f32[34,8,128]{2,1,0:T(8,128)S(1)} %copy-done.22), channel_id=1, source_target_pairs={{0,16},{1,17},{8,24},{9,25},{16,0},{17,1},{24,8},{25,9},{2,18},{3,... | collective-permute-start | bytes 417800 | tf_op jit(solution)/shard_map/ppermute | solution.py:437
  26.3 6.7 %collective-permute-start.14 = (f32[34,8,128]{2,1,0:T(8,128)S(1)}, f32[34,8,128]{2,1,0:T(8,128)S(1)}, u32[]{:S(2)}, u32[]{:S(2)}) collective-permute-start(f32[34,8,128]{2,1,0:T(8,128)S(1)} %copy-done.21), channel_id=1, source_target_pairs={{0,24},{1,25},{8,16},{9,17},{16,8},{17,9},{24,0},{25,1},{2,26},{3,... | collective-permute-start | bytes 417800 | tf_op jit(solution)/shard_map/ppermute | solution.py:437
  26.3 10.9 %collective-permute-start.2 = (f32[2,32,8,128]{3,2,1,0:T(8,128)S(1)}, f32[2,32,8,128]{3,2,1,0:T(8,128)S(1)}, u32[]{:S(2)}, u32[]{:S(2)}) collective-permute-start(f32[2,32,8,128]{3,2,1,0:T(8,128)S(1)} %get-tuple-element.42), channel_id=1, source_target_pairs={{0,9},{1,8},{8,1},{9,0},{16,25},{17,24},{24,17},{25,16},{2,11},{3,... | collective-permute-start | bytes 786440 | tf_op jit(solution)/shard_map/ppermute | solution.py:437
  30.9 20.4 %collective-permute-start.3 = (f32[2,32,8,128]{3,2,1,0:T(8,128)S(1)}, f32[2,32,8,128]{3,2,1,0:T(8,128)S(1)}, u32[]{:S(2)}, u32[]{:S(2)}) collective-permute-start(f32[2,32,8,128]{3,2,1,0:T(8,128)S(1)} %get-tuple-element.43), channel_id=1, source_target_pairs={{0,16},{1,17},{8,24},{9,25},{16,0},{17,1},{24,8},{25,9},{2,18},{3,... | collective-permute-start | bytes 786440 | tf_op jit(solution)/shard_map/ppermute | solution.py:437
  33.0 18.3 %collective-permute-start.4 = (f32[2,32,8,128]{3,2,1,0:T(8,128)S(1)}, f32[2,32,8,128]{3,2,1,0:T(8,128)S(1)}, u32[]{:S(2)}, u32[]{:S(2)}) collective-permute-start(f32[2,32,8,128]{3,2,1,0:T(8,128)S(1)} %get-tuple-element.44), channel_id=1, source_target_pairs={{0,17},{1,16},{8,25},{9,24},{16,1},{17,0},{24,9},{25,8},{2,19},{3,... | collective-permute-start | bytes 786440 | tf_op jit(solution)/shard_map/ppermute | solution.py:437
  33.9 20.7 %collective-permute-start.5 = (f32[2,32,8,128]{3,2,1,0:T(8,128)S(1)}, f32[2,32,8,128]{3,2,1,0:T(8,128)S(1)}, u32[]{:S(2)}, u32[]{:S(2)}) collective-permute-start(f32[2,32,8,128]{3,2,1,0:T(8,128)S(1)} %get-tuple-element.45), channel_id=1, source_target_pairs={{0,24},{1,25},{8,16},{9,17},{16,8},{17,9},{24,0},{25,1},{2,26},{3,... | collective-permute-start | bytes 786440 | tf_op jit(solution)/shard_map/ppermute | solution.py:437
  35.9 22.3 %collective-permute-start.6 = (f32[2,32,8,128]{3,2,1,0:T(8,128)S(1)}, f32[2,32,8,128]{3,2,1,0:T(8,128)S(1)}, u32[]{:S(2)}, u32[]{:S(2)}) collective-permute-start(f32[2,32,8,128]{3,2,1,0:T(8,128)S(1)} %get-tuple-element.46), channel_id=1, source_target_pairs={{0,25},{1,24},{8,17},{9,16},{16,9},{17,8},{24,1},{25,0},{2,27},{3,... | collective-permute-start | bytes 786440 | tf_op jit(solution)/shard_map/ppermute | solution.py:437
  37.1 59.7 %copy-start.10 = (bf16[16,96]{1,0:T(8,128)(2,1)S(1)}, bf16[16,96]{1,0:T(8,128)(2,1)}, u32[]{:S(2)}) copy-start(bf16[16,96]{1,0:T(8,128)(2,1)} %constant.29.clone.refs_8_) | copy-start | bytes 9220
  37.2 22.4 %collective-permute-start.16 = (f32[34,8,128]{2,1,0:T(8,128)S(1)}, f32[34,8,128]{2,1,0:T(8,128)S(1)}, u32[]{:S(2)}, u32[]{:S(2)}) collective-permute-start(f32[34,8,128]{2,1,0:T(8,128)S(1)} %copy-done.20), channel_id=1, source_target_pairs={{0,1},{1,0},{8,9},{9,8},{16,17},{17,16},{24,25},{25,24},{2,3},{3,2... | collective-permute-start | bytes 417800 | tf_op jit(solution)/shard_map/ppermute | solution.py:437
  51.4 9.3 %collective-permute-start.17 = (f32[34,8,128]{2,1,0:T(8,128)S(1)}, f32[34,8,128]{2,1,0:T(8,128)S(1)}, u32[]{:S(2)}, u32[]{:S(2)}) collective-permute-start(f32[34,8,128]{2,1,0:T(8,128)S(1)} %copy-done.19), channel_id=1, source_target_pairs={{0,8},{1,9},{8,0},{9,1},{16,24},{17,25},{24,16},{25,17},{2,10},{3,... | collective-permute-start | bytes 417800 | tf_op jit(solution)/shard_map/ppermute | solution.py:437
  51.4 11.4 %collective-permute-start.18 = (f32[34,8,128]{2,1,0:T(8,128)S(1)}, f32[34,8,128]{2,1,0:T(8,128)S(1)}, u32[]{:S(2)}, u32[]{:S(2)}) collective-permute-start(f32[34,8,128]{2,1,0:T(8,128)S(1)} %copy-done.18), channel_id=1, source_target_pairs={{0,9},{1,8},{8,1},{9,0},{16,25},{17,24},{24,17},{25,16},{2,11},{3,... | collective-permute-start | bytes 417800 | tf_op jit(solution)/shard_map/ppermute | solution.py:437
  54.6 27.4 %collective-permute-start.24 = (f32[4,34,8,128]{3,2,1,0:T(8,128)S(1)}, f32[4,34,8,128]{3,2,1,0:T(8,128)S(1)}, u32[]{:S(2)}, u32[]{:S(2)}) collective-permute-start(f32[4,34,8,128]{3,2,1,0:T(8,128)S(1)} %pad_maximum_fusion.1), channel_id=1, source_target_pairs={{0,2},{2,4},{3,1},{4,6},{5,3},{7,5},{8,10},{10,12},{11,9},{12,14},... | collective-permute-start | bytes 1671176 | tf_op jit(solution)/shard_map/ppermute | solution.py:461
  58.1 23.9 %collective-permute-start.23 = (f32[4,34,8,128]{3,2,1,0:T(8,128)S(1)}, f32[4,34,8,128]{3,2,1,0:T(8,128)S(1)}, u32[]{:S(2)}, u32[]{:S(2)}) collective-permute-start(f32[4,34,8,128]{3,2,1,0:T(8,128)S(1)} %pad_maximum_fusion), channel_id=1, source_target_pairs={{1,3},{2,0},{3,5},{4,2},{5,7},{6,4},{9,11},{10,8},{11,13},{12,10},... | collective-permute-start | bytes 1671176 | tf_op jit(solution)/shard_map/ppermute | solution.py:461
  59.6 9.6 %collective-permute-start.19 = (f32[34,8,128]{2,1,0:T(8,128)S(1)}, f32[34,8,128]{2,1,0:T(8,128)S(1)}, u32[]{:S(2)}, u32[]{:S(2)}) collective-permute-start(f32[34,8,128]{2,1,0:T(8,128)S(1)} %copy-done.17), channel_id=1, source_target_pairs={{0,16},{1,17},{8,24},{9,25},{16,0},{17,1},{24,8},{25,9},{2,18},{3,... | collective-permute-start | bytes 417800 | tf_op jit(solution)/shard_map/ppermute | solution.py:437
  60.7 13.1 %collective-permute-start.20 = (f32[34,8,128]{2,1,0:T(8,128)S(1)}, f32[34,8,128]{2,1,0:T(8,128)S(1)}, u32[]{:S(2)}, u32[]{:S(2)}) collective-permute-start(f32[34,8,128]{2,1,0:T(8,128)S(1)} %copy-done.16), channel_id=1, source_target_pairs={{0,17},{1,16},{8,25},{9,24},{16,1},{17,0},{24,9},{25,8},{2,19},{3,... | collective-permute-start | bytes 417800 | tf_op jit(solution)/shard_map/ppermute | solution.py:437
  62.8 12.2 %collective-permute-start.21 = (f32[34,8,128]{2,1,0:T(8,128)S(1)}, f32[34,8,128]{2,1,0:T(8,128)S(1)}, u32[]{:S(2)}, u32[]{:S(2)}) collective-permute-start(f32[34,8,128]{2,1,0:T(8,128)S(1)} %copy-done.15), channel_id=1, source_target_pairs={{0,24},{1,25},{8,16},{9,17},{16,8},{17,9},{24,0},{25,1},{2,26},{3,... | collective-permute-start | bytes 417800 | tf_op jit(solution)/shard_map/ppermute | solution.py:437
  69.2 31.7 %collective-permute-start.8 = (f32[4,32,4,128]{3,2,1,0:T(4,128)S(1)}, f32[4,32,4,128]{3,2,1,0:T(4,128)S(1)}, u32[]{:S(2)}, u32[]{:S(2)}) collective-permute-start(f32[4,32,4,128]{3,2,1,0:T(4,128)S(1)} %pad_maximum_fusion.3), channel_id=1, source_target_pairs={{0,2},{2,4},{3,1},{4,6},{5,3},{7,5},{8,10},{10,12},{11,9},{12,14},... | collective-permute-start | bytes 786440 | tf_op jit(solution)/shard_map/ppermute | solution.py:461
  73.8 27.1 %collective-permute-start.7 = (f32[4,32,4,128]{3,2,1,0:T(4,128)S(1)}, f32[4,32,4,128]{3,2,1,0:T(4,128)S(1)}, u32[]{:S(2)}, u32[]{:S(2)}) collective-permute-start(f32[4,32,4,128]{3,2,1,0:T(4,128)S(1)} %pad_maximum_fusion.2), channel_id=1, source_target_pairs={{1,3},{2,0},{3,5},{4,2},{5,7},{6,4},{9,11},{10,8},{11,13},{12,10},... | collective-permute-start | bytes 786440 | tf_op jit(solution)/shard_map/ppermute | solution.py:461
  75.1 6.9 %collective-permute-start.22 = (f32[34,8,128]{2,1,0:T(8,128)S(1)}, f32[34,8,128]{2,1,0:T(8,128)S(1)}, u32[]{:S(2)}, u32[]{:S(2)}) collective-permute-start(f32[34,8,128]{2,1,0:T(8,128)S(1)} %copy-done.14), channel_id=1, source_target_pairs={{0,25},{1,24},{8,17},{9,16},{16,9},{17,8},{24,1},{25,0},{2,27},{3,... | collective-permute-start | bytes 417800 | tf_op jit(solution)/shard_map/ppermute | solution.py:437
  105.6 4.0 %collective-permute-start.25 = (f32[4,16,128]{2,1,0:T(8,128)S(1)}, f32[4,16,128]{2,1,0:T(8,128)S(1)}, u32[]{:S(2)}, u32[]{:S(2)}) collective-permute-start(f32[4,16,128]{2,1,0:T(8,128)S(1)} %get-tuple-element.67), channel_id=1, source_target_pairs={{0,1},{1,0},{2,3},{3,2},{4,5},{5,4},{6,7},{7,6},{8,9},{9,8},{10,11... | collective-permute-start | bytes 98312 | tf_op jit(solution)/shard_map/ppermute | solution.py:570
  (18 other events, 409.0 us)
where the time goes:
time: 110 us
  Pallas kernels  36.1 us (33%)
  starting transfers between devices  34.7 us (32%)
  waiting for transfers between devices  33.7 us (31%)
  local copies, waits for them, and re-layouts  2.94 us (3%)
  other arithmetic  2.3 us (2%)
    ppermute x21, waiting for transfers between devices, exchange(): got[m] = lax.ppermute(blocks[m], GROUP, pairs)  30.4 us
    ppermute x21, starting transfers between devices, exchange(): got[m] = lax.ppermute(blocks[m], GROUP, pairs)  23.3 us
    pallas_call x1, Pallas kernels, colours(): vmem_call(functools.partial(first_kernel, groups, slab, extra, blocks, co...  14.7 us
    pallas_call x2, Pallas kernels, source(): pl.pallas_call(functools.partial(source_kernel, blocks, groups, which, ex...  12.7 us
    ppermute x4, starting transfers between devices, row_halo(): found.append(lax.ppermute(jnp.stack(edge), ('strips', 'pair'), pairs))  10.6 us
    pallas_call x2, Pallas kernels, march(): vmem_call(functools.partial(second_kernel, groups, slab, blocks, bool(hal...  8.67 us
    ppermute x1, waiting for transfers between devices, local(): given = lax.ppermute(image[1], 'pair', [(0, 1), (1, 0)])  3.26 us
    unnamed x48, local copies, waits for them, and re-layouts  2.29 us
  transfers between devices with their start and end apart: 26, of which 8 were waited for; matrix products, arithmetic and copies ran while one was open for 2% of the time, Pallas kernels for 20%

commit v1 on v0

--- a/solution.py
+++ b/solution.py
@@ -65,8 +65,8 @@
 
 
 def source_kernel(blocks, groups, which, edges, planes, *refs):
-    fields_ref, bh_ref, bl_ref = refs[:3]
-    outs, (held, us, in_sems, sems) = refs[3:-4], refs[-4:]
+    fields_ref, bands_ref = refs[:2]
+    outs, (held, bands, us, ev, in_sems, sems) = refs[2:-6], refs[-6:]
     if edges:
         flag_ref, outs = outs[-1], outs[:-1]
     joined = len(outs) == blocks
@@ -78,7 +78,10 @@
         part = pl.ds(step * planes, planes)
         return pltpu.make_async_copy(fields_ref.at[which, part], held.at[part], in_sems.at[step])
 
-    for step in range(steps):
+    matrices = pltpu.make_async_copy(bands_ref, bands, in_sems.at[steps])
+    fetch(0).start()
+    matrices.start()
+    for step in range(1, steps):
         fetch(step).start()
 
     def filtered(step):
@@ -87,8 +90,8 @@
         for j in range(columns // wide):
             left, right = max(0, wide * j - LANES), min(columns, wide * (j + 1) + LANES)
             base = left - (wide * j - LANES)
-            bh = bh_ref[base : base + right - left]
-            bl = bl_ref[base : base + right - left]
+            bh = bands[0, base : base + right - left]
+            bl = bands[1, base : base + right - left]
             u = mxu(hi[:, left:right], bh) + mxu(lo[:, left:right], bh) + mxu(hi[:, left:right], bl)
             for h in range(2):
                 us[2 * j + h, pl.ds(step * planes, planes)] = u[
@@ -101,7 +104,7 @@
     if edges:
         flag_ref[...] = jnp.zeros(flag_ref.shape, jnp.float32) + (place == groups - 1).astype(jnp.float32)
 
-    def copies(at, first, count):
+    def copies(at, origin, start, first, count):
         found = []
         for m in range(blocks):
             for h in range(2):
@@ -109,7 +112,7 @@
                 target = outs[m].at[h] if joined else outs[h * blocks + m]
                 found.append(
                     pltpu.make_async_copy(
-                        us.at[me ^ m, pl.ds(first, count), pl.ds(row, HALO)],
+                        origin.at[me ^ m, pl.ds(start, count), pl.ds(row, HALO)],
                         target.at[pl.ds(first, count)],
                         sems.at[at, 2 * m + h],
                     )
@@ -120,38 +123,39 @@
         lane = lax.broadcasted_iota(jnp.int32, (rows, LANES), 1)
         zero = jnp.zeros((rows, LANES), jnp.float32)
         part = lax.rem(step, PER // planes) * planes
-        at = slab + step * planes // PER
+        at = step * planes // PER
         for b in range(blocks):
-            acc = us[b, at]
+            acc = ev[b, at]
             for z in range(planes):
                 before = us[b - 1, step * planes + z] if b > 0 else zero
                 after = us[b + 1, step * planes + z] if b < blocks - 1 else zero
                 both = jnp.where(lane >= LANES // 2, before, after)
                 moved = pltpu.roll(both, lax.rem(RAD + 2 * RAD * (z + part), LANES), 1)
                 acc = jnp.where(lane // (2 * RAD) == z + part, moved, acc)
-            us[b, at] = acc
+            ev[b, at] = acc
 
     def body(step, carry):
         fetch(step).wait()
         filtered(step)
-        for copy in copies(step, step * planes, planes):
+        for copy in copies(step, us, step * planes, step * planes, planes):
             copy.start()
         if edges:
             collected(step)
         return carry
 
+    matrices.wait()
     lax.fori_loop(0, steps, body, 0)
-    last = copies(steps, slab, edges) if edges else []
+    last = copies(steps, ev, 0, slab, edges) if edges else []
     for copy in last:
         copy.start()
     for at in range(steps):
-        for copy in copies(at, at * planes, planes):
+        for copy in copies(at, us, at * planes, at * planes, planes):
             copy.wait()
     for copy in last:
         copy.wait()
 
 
-def source(fields, which, groups, bh, bl, edges, joined, vmem):
+def source(fields, which, groups, bands, edges, joined, vmem):
     _, slab, rows, columns = fields.shape
     blocks = columns // LANES
     extra = slab // PER if edges else 0
@@ -163,19 +167,21 @@
     flag_shape = [(8, LANES)] if edges else []
     return pl.pallas_call(
         functools.partial(source_kernel, blocks, groups, which, extra, planes),
-        in_specs=[pl.BlockSpec(memory_space=pltpu.HBM)] + [pl.BlockSpec(memory_space=pltpu.VMEM)] * 2,
+        in_specs=[pl.BlockSpec(memory_space=pltpu.HBM)] * 2,
         out_specs=[pl.BlockSpec(memory_space=pl.ANY)] * len(shapes) + flag_spec,
         out_shape=[jax.ShapeDtypeStruct(shape, jnp.float32) for shape in shapes + flag_shape],
         scratch_shapes=[
             pltpu.VMEM((slab, rows, columns), jnp.float32),
-            pltpu.VMEM((blocks, slab + extra, rows, LANES), jnp.float32),
-            pltpu.SemaphoreType.DMA((steps,)),
+            pltpu.VMEM(bands.shape, jnp.bfloat16),
+            pltpu.VMEM((blocks, slab, rows, LANES), jnp.float32),
+            pltpu.VMEM((blocks, max(extra, 1), rows, LANES), jnp.float32),
+            pltpu.SemaphoreType.DMA((steps + 1,)),
             pltpu.SemaphoreType.DMA((steps + 1, 2 * blocks)),
         ],
         compiler_params=pltpu.CompilerParams(vmem_limit_bytes=vmem),
         cost_estimate=cost(5),
         name="columns_filter",
-    )(fields, bh, bl)
+    )(fields, bands)
 
 
 def cost(microseconds):
@@ -476,7 +482,7 @@
     bins = tf_index.shape[0]
     blocks = depth * groups
 
-    bh, bl = split_np(band(S_TAPS, 2 * LANES, 4 * LANES, LANES).T)
+    bands = jnp.asarray(np.stack(split_np(band(S_TAPS, 2 * LANES, 4 * LANES, LANES).T)))
     smooth_rows = band(S_TAPS, rows + 2 * RAD, wide, HALO - RAD)
     slope_rows = band(D_TAPS, rows, rows + 2 * RAD, RAD)
     inner = slice(HALO, rows - HALO)
@@ -552,11 +558,10 @@
         )(*own, *halos, lhs, coloured, *others)
 
     order = sorted(range(1, blocks), key=lambda m: (bin(m).count("1"), m))
-    sent0 = list(source(fields, 0, groups, bh, bl, True, False, 60 << 20))
+    sent0 = list(source(fields, 0, groups, bands, True, False, 60 << 20))
     leads = sent0.pop()[0] > 0.5
     got0 = exchange(sent0[:blocks], order) + exchange(sent0[blocks:], order)
-    bh, pair, palette = lax.optimization_barrier((jnp.asarray(bh), pair, palette))
-    sent1 = source(fields, 1, groups, bh, bl, False, True, 16 << 20)
+    sent1 = source(fields, 1, groups, bands, False, True, 58 << 20)
     halo0 = row_halo(got0, groups, count, leads)
     got1 = exchange(sent1, order)
     halo1 = row_halo(got1, groups, count, leads)

time: 110 us -> 105 us (0.955)
  waiting for transfers between devices: 33.7 us -> 31.2 us
  local copies, waits for them, and re-layouts: 2.94 us -> 0.76 us
  Pallas kernels: 36.1 us -> 34.6 us
    ppermute x21, waiting for transfers between devices: 30.4 us -> 18.4 us  [exchange(): got[m] = lax.ppermute(blocks[m], GROUP, pairs)]
    ppermute x4, waiting for transfers between devices: 0.01 us -> 8.91 us  [row_halo(): found.append(lax.ppermute(jnp.stack(edge), ('strips', 'pair'), pairs))]
    unnamed x48 -> x44, local copies, waits for them, and re-layouts: 2.29 us -> 0.1 us
    ppermute x21, starting transfers between devices: 23.3 us -> 24.9 us  [exchange(): got[m] = lax.ppermute(blocks[m], GROUP, pairs)]
    pallas_call x2, Pallas kernels: 12.7 us -> 11.3 us  [source(): pl.pallas_call(functools.partial(source_kernel, blocks, groups, which, ex...]
    ppermute x4, starting transfers between devices: 10.6 us -> 9.54 us  [row_halo(): found.append(lax.ppermute(jnp.stack(edge), ('strips', 'pair'), pairs))]
  transfers between devices with their start and end apart: 26 -> 26, of which waited for: 8 -> 9; matrix products, arithmetic and copies ran while one was open for 2% -> 3% of each run, Pallas kernels for 20% -> 23%
where the time goes in v1:
time: 105 us
  Pallas kernels  34.6 us (33%)
  starting transfers between devices  34.6 us (33%)
  waiting for transfers between devices  31.2 us (30%)
  other arithmetic  3.37 us (3%)
    ppermute x21, starting transfers between devices, exchange(): got[m] = lax.ppermute(blocks[m], GROUP, pairs)  24.9 us
    ppermute x21, waiting for transfers between devices, exchange(): got[m] = lax.ppermute(blocks[m], GROUP, pairs)  18.4 us
    pallas_call x1, Pallas kernels, colours(): vmem_call(functools.partial(first_kernel, groups, slab, extra, blocks, co...  14.6 us
    pallas_call x2, Pallas kernels, source(): pl.pallas_call(functools.partial(source_kernel, blocks, groups, which, ex...  11.3 us
    ppermute x4, starting transfers between devices, row_halo(): found.append(lax.ppermute(jnp.stack(edge), ('strips', 'pair'), pairs))  9.54 us
    ppermute x4, waiting for transfers between devices, row_halo(): found.append(lax.ppermute(jnp.stack(edge), ('strips', 'pair'), pairs))  8.91 us
    pallas_call x2, Pallas kernels, march(): vmem_call(functools.partial(second_kernel, groups, slab, blocks, bool(hal...  8.67 us
    ppermute x1, waiting for transfers between devices, local(): given = lax.ppermute(image[1], 'pair', [(0, 1), (1, 0)])  3.9 us
  transfers between devices with their start and end apart: 26, of which 9 were waited for; matrix products, arithmetic and copies ran while one was open for 3% of the time, Pallas kernels for 23%

profile of v1, /device:TPU:0, one launch (start us, length us, event | category | flops | bytes accessed | tf_op | source)
XLA Modules:
  0.0 104.9 jit_solution(11446387450709387956)
XLA Ops:
  0.0 6.2 %columns_filter.2 = (f32[34,8,128]{2,1,0:T(8,128)}, f32[34,8,128]{2,1,0:T(8,128)}, f32[34,8,128]{2,1,0:T(8,128)}, f32[34,8,128]{2,1,0:T(8,128)}, f32[34,8,128]{2...) custom-call(f32[2,32,16,1024]{3,2,1,0:T(8,128)} %refs_0_.3, ...), custom_call_target="tpu_custom_call" | custom-call | bytes 15000000 | tf_op jit(solution)/shard_map/columns_filter/pallas_call | solution.py:168
  6.3 3.0 %collective-permute-start.9 = (f32[34,8,128]{2,1,0:T(8,128)}, f32[34,8,128]{2,1,0:T(8,128)S(1)}, u32[]{:S(2)}, u32[]{:S(2)}) collective-permute-start(f32[34,8,128]{2,1,0:T(8,128)} %get-tuple-element.44), channel_id=1, source_target_pairs={{0,1},{1,0},{8,9},{9,8},{16,17},{17,16},{24,25},{25,24},{2,3},{3,2... | collective-permute-start | bytes 417800 | tf_op jit(solution)/shard_map/ppermute | solution.py:443
  9.3 2.1 %collective-permute-start.13 = (f32[34,8,128]{2,1,0:T(8,128)}, f32[34,8,128]{2,1,0:T(8,128)S(1)}, u32[]{:S(2)}, u32[]{:S(2)}) collective-permute-start(f32[34,8,128]{2,1,0:T(8,128)} %get-tuple-element.48), channel_id=1, source_target_pairs={{0,17},{1,16},{8,25},{9,24},{16,1},{17,0},{24,9},{25,8},{2,19},{3,... | collective-permute-start | bytes 417800 | tf_op jit(solution)/shard_map/ppermute | solution.py:443
  12.1 5.1 %columns_filter.3 = (f32[2,32,8,128]{3,2,1,0:T(8,128)}, f32[2,32,8,128]{3,2,1,0:T(8,128)}, f32[2,32,8,128]{3,2,1,0:T(8,128)}, f32[2,32,8,128]{3,2,1,0:T(8,128)},...) custom-call(f32[2,32,16,1024]{3,2,1,0:T(8,128)} %refs_0_.3, ...), custom_call_target="tpu_custom_call" | custom-call | bytes 15000000 | tf_op jit(solution)/shard_map/columns_filter/pallas_call | solution.py:168
  17.3 1.7 %collective-permute-start = (f32[2,32,8,128]{3,2,1,0:T(8,128)}, f32[2,32,8,128]{3,2,1,0:T(8,128)S(1)}, u32[]{:S(2)}, u32[]{:S(2)}) collective-permute-start(f32[2,32,8,128]{3,2,1,0:T(8,128)} %get-tuple-element.36), channel_id=1, source_target_pairs={{0,1},{1,0},{8,9},{9,8},{16,17},{17,16},{24,25},{25,24},{2,3},{3,2... | collective-permute-start | bytes 786440 | tf_op jit(solution)/shard_map/ppermute | solution.py:443
  19.5 1.7 %collective-permute-done.13.refs_5_ = f32[34,8,128]{2,1,0:T(8,128)S(1)} collective-permute-done((f32[34,8,128]{2,1,0:T(8,128)}, f32[34,8,128]{2,1,0:T(8,128)S(1)}, u32[]{:S(2)}, u32[]{:S(2)}) %collective-permute-start.13) | collective-permute-done | bytes 139296 | tf_op jit(solution)/shard_map/ppermute | solution.py:443
  21.3 1.3 %collective-permute-done.15.refs_7_ = f32[34,8,128]{2,1,0:T(8,128)S(1)} collective-permute-done((f32[34,8,128]{2,1,0:T(8,128)}, f32[34,8,128]{2,1,0:T(8,128)S(1)}, u32[]{:S(2)}, u32[]{:S(2)}) %collective-permute-start.15) | collective-permute-done | bytes 139296 | tf_op jit(solution)/shard_map/ppermute | solution.py:443
  22.6 1.1 %collective-permute-start.14 = (f32[34,8,128]{2,1,0:T(8,128)S(1)}, f32[34,8,128]{2,1,0:T(8,128)S(1)}, u32[]{:S(2)}, u32[]{:S(2)}) collective-permute-start(f32[34,8,128]{2,1,0:T(8,128)S(1)} %copy-done.19), channel_id=1, source_target_pairs={{0,24},{1,25},{8,16},{9,17},{16,8},{17,9},{24,0},{25,1},{2,26},{3,... | collective-permute-start | bytes 417800 | tf_op jit(solution)/shard_map/ppermute | solution.py:443
  23.7 1.8 %collective-permute-start.2 = (f32[2,32,8,128]{3,2,1,0:T(8,128)}, f32[2,32,8,128]{3,2,1,0:T(8,128)S(1)}, u32[]{:S(2)}, u32[]{:S(2)}) collective-permute-start(f32[2,32,8,128]{3,2,1,0:T(8,128)} %get-tuple-element.38), channel_id=1, source_target_pairs={{0,9},{1,8},{8,1},{9,0},{16,25},{17,24},{24,17},{25,16},{2,11},{3,... | collective-permute-start | bytes 786440 | tf_op jit(solution)/shard_map/ppermute | solution.py:443
  25.5 1.6 %collective-permute-done.12.refs_4_ = f32[34,8,128]{2,1,0:T(8,128)S(1)} collective-permute-done((f32[34,8,128]{2,1,0:T(8,128)S(1)}, f32[34,8,128]{2,1,0:T(8,128)S(1)}, u32[]{:S(2)}, u32[]{:S(2)}) %collective-permute-start.12) | collective-permute-done | bytes 139296 | tf_op jit(solution)/shard_map/ppermute | solution.py:443
  27.1 1.3 %collective-permute-done.14.refs_6_ = f32[34,8,128]{2,1,0:T(8,128)S(1)} collective-permute-done((f32[34,8,128]{2,1,0:T(8,128)S(1)}, f32[34,8,128]{2,1,0:T(8,128)S(1)}, u32[]{:S(2)}, u32[]{:S(2)}) %collective-permute-start.14) | collective-permute-done | bytes 139296 | tf_op jit(solution)/shard_map/ppermute | solution.py:443
  28.4 2.5 %collective-permute-start.4 = (f32[2,32,8,128]{3,2,1,0:T(8,128)}, f32[2,32,8,128]{3,2,1,0:T(8,128)S(1)}, u32[]{:S(2)}, u32[]{:S(2)}) collective-permute-start(f32[2,32,8,128]{3,2,1,0:T(8,128)} %get-tuple-element.40), channel_id=1, source_target_pairs={{0,17},{1,16},{8,25},{9,24},{16,1},{17,0},{24,9},{25,8},{2,19},{3,... | collective-permute-start | bytes 786440 | tf_op jit(solution)/shard_map/ppermute | solution.py:443
  30.9 1.9 %collective-permute-start.5 = (f32[2,32,8,128]{3,2,1,0:T(8,128)}, f32[2,32,8,128]{3,2,1,0:T(8,128)S(1)}, u32[]{:S(2)}, u32[]{:S(2)}) collective-permute-start(f32[2,32,8,128]{3,2,1,0:T(8,128)} %get-tuple-element.41), channel_id=1, source_target_pairs={{0,24},{1,25},{8,16},{9,17},{16,8},{17,9},{24,0},{25,1},{2,26},{3,... | collective-permute-start | bytes 786440 | tf_op jit(solution)/shard_map/ppermute | solution.py:443
  34.3 1.6 %collective-permute-start.16 = (f32[34,8,128]{2,1,0:T(8,128)S(1)}, f32[34,8,128]{2,1,0:T(8,128)S(1)}, u32[]{:S(2)}, u32[]{:S(2)}) collective-permute-start(f32[34,8,128]{2,1,0:T(8,128)S(1)} %copy-done.18), channel_id=1, source_target_pairs={{0,1},{1,0},{8,9},{9,8},{16,17},{17,16},{24,25},{25,24},{2,3},{3,2... | collective-permute-start | bytes 417800 | tf_op jit(solution)/shard_map/ppermute | solution.py:443
  35.9 11.1 %collective-permute-done.3.refs_4_ = f32[2,32,8,128]{3,2,1,0:T(8,128)S(1)} collective-permute-done((f32[2,32,8,128]{3,2,1,0:T(8,128)}, f32[2,32,8,128]{3,2,1,0:T(8,128)S(1)}, u32[]{:S(2)}, u32[]{:S(2)}) %collective-permute-start.3) | collective-permute-done | bytes 262176 | tf_op jit(solution)/shard_map/ppermute | solution.py:443
  47.0 2.7 %collective-permute-start.18 = (f32[34,8,128]{2,1,0:T(8,128)S(1)}, f32[34,8,128]{2,1,0:T(8,128)S(1)}, u32[]{:S(2)}, u32[]{:S(2)}) collective-permute-start(f32[34,8,128]{2,1,0:T(8,128)S(1)} %copy-done.16), channel_id=1, source_target_pairs={{0,9},{1,8},{8,1},{9,0},{16,25},{17,24},{24,17},{25,16},{2,11},{3,... | collective-permute-start | bytes 417800 | tf_op jit(solution)/shard_map/ppermute | solution.py:443
  49.7 1.3 %collective-permute-done.5.refs_6_ = f32[2,32,8,128]{3,2,1,0:T(8,128)S(1)} collective-permute-done((f32[2,32,8,128]{3,2,1,0:T(8,128)}, f32[2,32,8,128]{3,2,1,0:T(8,128)S(1)}, u32[]{:S(2)}, u32[]{:S(2)}) %collective-permute-start.5) | collective-permute-done | bytes 262176 | tf_op jit(solution)/shard_map/ppermute | solution.py:443
  51.0 1.3 %collective-permute-start.19 = (f32[34,8,128]{2,1,0:T(8,128)S(1)}, f32[34,8,128]{2,1,0:T(8,128)S(1)}, u32[]{:S(2)}, u32[]{:S(2)}) collective-permute-start(f32[34,8,128]{2,1,0:T(8,128)S(1)} %copy-done.15), channel_id=1, source_target_pairs={{0,16},{1,17},{8,24},{9,25},{16,0},{17,1},{24,8},{25,9},{2,18},{3,... | collective-permute-start | bytes 417800 | tf_op jit(solution)/shard_map/ppermute | solution.py:443
  52.3 0.9 collective-permute-start.20
  53.3 1.1 %slice_select_fusion.3 = (f32[1,32,4,128]{3,2,1,0:T(4,128)S(1)}, f32[1,32,4,128]{3,2,1,0:T(4,128)S(1)}, f32[1,32,4,128]{3,2,1,0:T(4,128)S(1)}, f32[1,32,4,128]{3...) fusion(f32[2,32,8,128]{3,2,1,0:T(8,128)S(1)} %collective-permut, ...), kind=kLoop, calls=%fused_computation.7 | loop fusion | flops 131072 | bytes 1572992 | tf_op jit(solution)/shard_map/jit(_where)/select_n | solution.py:458
  54.4 1.5 %collective-permute-start.21 = (f32[34,8,128]{2,1,0:T(8,128)S(1)}, f32[34,8,128]{2,1,0:T(8,128)S(1)}, u32[]{:S(2)}, u32[]{:S(2)}) collective-permute-start(f32[34,8,128]{2,1,0:T(8,128)S(1)} %copy-done.13), channel_id=1, source_target_pairs={{0,24},{1,25},{8,16},{9,17},{16,8},{17,9},{24,0},{25,1},{2,26},{3,... | collective-permute-start | bytes 417800 | tf_op jit(solution)/shard_map/ppermute | solution.py:443
  55.9 3.5 %collective-permute-start.24 = (f32[4,34,8,128]{3,2,1,0:T(8,128)S(1)}, f32[4,34,8,128]{3,2,1,0:T(8,128)S(1)}, u32[]{:S(2)}, u32[]{:S(2)}) collective-permute-start(f32[4,34,8,128]{3,2,1,0:T(8,128)S(1)} %pad_maximum_fusion.1), channel_id=1, source_target_pairs={{0,2},{2,4},{3,1},{4,6},{5,3},{7,5},{8,10},{10,12},{11,9},{12,14},... | collective-permute-start | bytes 1671176 | tf_op jit(solution)/shard_map/ppermute | solution.py:467
  59.5 1.3 %collective-permute-start.23 = (f32[4,34,8,128]{3,2,1,0:T(8,128)S(1)}, f32[4,34,8,128]{3,2,1,0:T(8,128)S(1)}, u32[]{:S(2)}, u32[]{:S(2)}) collective-permute-start(f32[4,34,8,128]{3,2,1,0:T(8,128)S(1)} %pad_maximum_fusion), channel_id=1, source_target_pairs={{1,3},{2,0},{3,5},{4,2},{5,7},{6,4},{9,11},{10,8},{11,13},{12,10},... | collective-permute-start | bytes 1671176 | tf_op jit(solution)/shard_map/ppermute | solution.py:467
  60.9 1.5 %collective-permute-start.22 = (f32[34,8,128]{2,1,0:T(8,128)S(1)}, f32[34,8,128]{2,1,0:T(8,128)S(1)}, u32[]{:S(2)}, u32[]{:S(2)}) collective-permute-start(f32[34,8,128]{2,1,0:T(8,128)S(1)} %copy-done.12), channel_id=1, source_target_pairs={{0,25},{1,24},{8,17},{9,16},{16,9},{17,8},{24,1},{25,0},{2,27},{3,... | collective-permute-start | bytes 417800 | tf_op jit(solution)/shard_map/ppermute | solution.py:443
  62.4 3.5 %collective-permute-start.8 = (f32[4,32,4,128]{3,2,1,0:T(4,128)S(1)}, f32[4,32,4,128]{3,2,1,0:T(4,128)S(1)}, u32[]{:S(2)}, u32[]{:S(2)}) collective-permute-start(f32[4,32,4,128]{3,2,1,0:T(4,128)S(1)} %pad_maximum_fusion.3), channel_id=1, source_target_pairs={{0,2},{2,4},{3,1},{4,6},{5,3},{7,5},{8,10},{10,12},{11,9},{12,14},... | collective-permute-start | bytes 786440 | tf_op jit(solution)/shard_map/ppermute | solution.py:467
  65.9 1.3 %collective-permute-start.7 = (f32[4,32,4,128]{3,2,1,0:T(4,128)S(1)}, f32[4,32,4,128]{3,2,1,0:T(4,128)S(1)}, u32[]{:S(2)}, u32[]{:S(2)}) collective-permute-start(f32[4,32,4,128]{3,2,1,0:T(4,128)S(1)} %pad_maximum_fusion.2), channel_id=1, source_target_pairs={{1,3},{2,0},{3,5},{4,2},{5,7},{6,4},{9,11},{10,8},{11,13},{12,10},... | collective-permute-start | bytes 786440 | tf_op jit(solution)/shard_map/ppermute | solution.py:467
  67.9 4.5 %collective-permute-done.24.refs_17_ = f32[4,34,8,128]{3,2,1,0:T(8,128)S(1)} collective-permute-done((f32[4,34,8,128]{3,2,1,0:T(8,128)S(1)}, f32[4,34,8,128]{3,2,1,0:T(8,128)S(1)}, u32[]{:S(2)}, u32[]{:S(2)}) %collective-permute-start.24) | collective-permute-done | bytes 557088 | tf_op jit(solution)/shard_map/ppermute | solution.py:467
  72.4 4.4 %collective-permute-done.23.refs_16_ = f32[4,34,8,128]{3,2,1,0:T(8,128)S(1)} collective-permute-done((f32[4,34,8,128]{3,2,1,0:T(8,128)S(1)}, f32[4,34,8,128]{3,2,1,0:T(8,128)S(1)}, u32[]{:S(2)}, u32[]{:S(2)}) %collective-permute-start.23) | collective-permute-done | bytes 557088 | tf_op jit(solution)/shard_map/ppermute | solution.py:467
  76.9 14.6 %shard_map.109 = (f32[4,128,16,128]{3,2,1,0:T(8,128)S(1)}, f32[4,128,16,128]{3,2,1,0:T(8,128)S(1)}) custom-call(f32[34,8,128]{2,1,0:T(8,128)S(1)} %copy-done.1, f32[34,8,128]{2,1,0:T(8,128)S(1)} %collective-permute-done.9.refs_1_, f32[34,8,128]{2,1,0:T(8,128)S(1)} %collective-permute-done.10.refs_2_, f32[34,8,128]{2,1,0:T(8,128)S(1)} %collective-permute-done.11.refs_3_, ...), custom_call_target="tpu_custom_call" | custom-call | bytes 60000000 | tf_op jit(solution)/shard_map/pallas_call | solution.py:526
  91.5 4.0 %shard_map.110.refs_12_ = f32[4,16,128]{2,1,0:T(8,128)S(1)} custom-call(f32[2,32,8,128]{3,2,1,0:T(8,128)S(1)} %copy-done, f32[2,32,8,128]{3,2,1,0:T(8,128)S(1)} %collective-permute-done.refs_1_, f32[2,32,8,128]{3,2,1,0:T(8,128)S(1)} %collective-permute-done.1.refs_2_, f32[2,32,8,128]{3,2,1,0:T(8,128)S(1)} %collective-permute-done.2.refs_3_, ...), custom_call_target="tpu_custom_call" | custom-call | bytes 15000000 | tf_op jit(solution)/shard_map/pallas_call | solution.py:547
  95.6 4.6 %shard_map.111 = (f32[4,16,128]{2,1,0:T(8,128)S(1)}, f32[4,16,128]{2,1,0:T(8,128)S(1)}) custom-call(f32[2,32,8,128]{3,2,1,0:T(8,128)S(1)} %copy-done, f32[2,32,8,128]{3,2,1,0:T(8,128)S(1)} %collective-permute-done.refs_1_, f32[2,32,8,128]{3,2,1,0:T(8,128)S(1)} %collective-permute-done.1.refs_2_, f32[2,32,8,128]{3,2,1,0:T(8,128)S(1)} %collective-permute-done.2.refs_3_, ...), custom_call_target="tpu_custom_call" | custom-call | bytes 15000000 | tf_op jit(solution)/shard_map/pallas_call | solution.py:547
  100.3 3.9 %collective-permute-done.25 = f32[4,16,128]{2,1,0:T(8,128)S(1)} collective-permute-done((f32[4,16,128]{2,1,0:T(8,128)S(1)}, f32[4,16,128]{2,1,0:T(8,128)S(1)}, u32[]{:S(2)}, u32[]{:S(2)}) %collective-permute-start.25) | collective-permute-done | bytes 32800 | tf_op jit(solution)/shard_map/ppermute | solution.py:575
  (81 shorter events, 4.3 us)
Async XLA Ops:
  6.3 12.8 %collective-permute-start.9 = (f32[34,8,128]{2,1,0:T(8,128)}, f32[34,8,128]{2,1,0:T(8,128)S(1)}, u32[]{:S(2)}, u32[]{:S(2)}) collective-permute-start(f32[34,8,128]{2,1,0:T(8,128)} %get-tuple-element.44), channel_id=1, source_target_pairs={{0,1},{1,0},{8,9},{9,8},{16,17},{17,16},{24,25},{25,24},{2,3},{3,2... | collective-permute-start | bytes 417800 | tf_op jit(solution)/shard_map/ppermute | solution.py:443
  9.3 9.7 %collective-permute-start.11 = (f32[34,8,128]{2,1,0:T(8,128)}, f32[34,8,128]{2,1,0:T(8,128)S(1)}, u32[]{:S(2)}, u32[]{:S(2)}) collective-permute-start(f32[34,8,128]{2,1,0:T(8,128)} %get-tuple-element.46), channel_id=1, source_target_pairs={{0,9},{1,8},{8,1},{9,0},{16,25},{17,24},{24,17},{25,16},{2,11},{3,... | collective-permute-start | bytes 417800 | tf_op jit(solution)/shard_map/ppermute | solution.py:443
  9.3 12.0 %collective-permute-start.13 = (f32[34,8,128]{2,1,0:T(8,128)}, f32[34,8,128]{2,1,0:T(8,128)S(1)}, u32[]{:S(2)}, u32[]{:S(2)}) collective-permute-start(f32[34,8,128]{2,1,0:T(8,128)} %get-tuple-element.48), channel_id=1, source_target_pairs={{0,17},{1,16},{8,25},{9,24},{16,1},{17,0},{24,9},{25,8},{2,19},{3,... | collective-permute-start | bytes 417800 | tf_op jit(solution)/shard_map/ppermute | solution.py:443
  11.4 65.4 %copy-start.2 = (f32[34,8,128]{2,1,0:T(8,128)S(1)}, f32[34,8,128]{2,1,0:T(8,128)}, u32[]{:S(2)}) copy-start(f32[34,8,128]{2,1,0:T(8,128)} %get-tuple-element.51.refs_8_) | copy-start | bytes 417796
  11.4 65.4 %copy-start.3 = (bf16[4,64,144]{2,1,0:T(8,128)(2,1)S(1)}, bf16[4,64,144]{2,1,0:T(8,128)(2,1)}, u32[]{:S(2)}) copy-start(bf16[4,64,144]{2,1,0:T(8,128)(2,1)} %constant.22.clone.refs_18_) | copy-start | bytes 221188
  11.5 65.4 %copy-start.4 = (bf16[256,256]{1,0:T(8,128)(2,1)S(1)}, bf16[256,256]{1,0:T(8,128)(2,1)}, u32[]{:S(2)}) copy-start(bf16[256,256]{1,0:T(8,128)(2,1)} %constant.23.clone.refs_19_) | copy-start | bytes 393220
  11.5 65.4 %copy-start.5 = (bf16[384,128]{1,0:T(8,128)(2,1)S(1)}, bf16[384,128]{1,0:T(8,128)(2,1)}, u32[]{:S(2)}) copy-start(bf16[384,128]{1,0:T(8,128)(2,1)} %constant.24.clone.refs_20_) | copy-start | bytes 294916
  11.5 65.4 %copy-start.6 = (bf16[384,128]{1,0:T(8,128)(2,1)S(1)}, bf16[384,128]{1,0:T(8,128)(2,1)}, u32[]{:S(2)}) copy-start(bf16[384,128]{1,0:T(8,128)(2,1)} %constant.25.clone.refs_21_) | copy-start | bytes 294916
  11.5 11.1 %collective-permute-start.15 = (f32[34,8,128]{2,1,0:T(8,128)}, f32[34,8,128]{2,1,0:T(8,128)S(1)}, u32[]{:S(2)}, u32[]{:S(2)}) collective-permute-start(f32[34,8,128]{2,1,0:T(8,128)} %get-tuple-element.50), channel_id=1, source_target_pairs={{0,25},{1,24},{8,17},{9,16},{16,9},{17,8},{24,1},{25,0},{2,27},{3,... | collective-permute-start | bytes 417800 | tf_op jit(solution)/shard_map/ppermute | solution.py:443
  17.3 13.6 %collective-permute-start = (f32[2,32,8,128]{3,2,1,0:T(8,128)}, f32[2,32,8,128]{3,2,1,0:T(8,128)S(1)}, u32[]{:S(2)}, u32[]{:S(2)}) collective-permute-start(f32[2,32,8,128]{3,2,1,0:T(8,128)} %get-tuple-element.36), channel_id=1, source_target_pairs={{0,1},{1,0},{8,9},{9,8},{16,17},{17,16},{24,25},{25,24},{2,3},{3,2... | collective-permute-start | bytes 786440 | tf_op jit(solution)/shard_map/ppermute | solution.py:443
  19.0 13.8 %collective-permute-start.1 = (f32[2,32,8,128]{3,2,1,0:T(8,128)}, f32[2,32,8,128]{3,2,1,0:T(8,128)S(1)}, u32[]{:S(2)}, u32[]{:S(2)}) collective-permute-start(f32[2,32,8,128]{3,2,1,0:T(8,128)} %get-tuple-element.37), channel_id=1, source_target_pairs={{0,8},{1,9},{8,0},{9,1},{16,24},{17,25},{24,16},{25,17},{2,10},{3,... | collective-permute-start | bytes 786440 | tf_op jit(solution)/shard_map/ppermute | solution.py:443
  19.0 4.7 %collective-permute-start.10 = (f32[34,8,128]{2,1,0:T(8,128)S(1)}, f32[34,8,128]{2,1,0:T(8,128)S(1)}, u32[]{:S(2)}, u32[]{:S(2)}) collective-permute-start(f32[34,8,128]{2,1,0:T(8,128)S(1)} %copy-done.21), channel_id=1, source_target_pairs={{0,8},{1,9},{8,0},{9,1},{16,24},{17,25},{24,16},{25,17},{2,10},{3,... | collective-permute-start | bytes 417800 | tf_op jit(solution)/shard_map/ppermute | solution.py:443
  21.3 5.8 %collective-permute-start.12 = (f32[34,8,128]{2,1,0:T(8,128)S(1)}, f32[34,8,128]{2,1,0:T(8,128)S(1)}, u32[]{:S(2)}, u32[]{:S(2)}) collective-permute-start(f32[34,8,128]{2,1,0:T(8,128)S(1)} %copy-done.20), channel_id=1, source_target_pairs={{0,16},{1,17},{8,24},{9,25},{16,0},{17,1},{24,8},{25,9},{2,18},{3,... | collective-permute-start | bytes 417800 | tf_op jit(solution)/shard_map/ppermute | solution.py:443
  22.6 5.8 %collective-permute-start.14 = (f32[34,8,128]{2,1,0:T(8,128)S(1)}, f32[34,8,128]{2,1,0:T(8,128)S(1)}, u32[]{:S(2)}, u32[]{:S(2)}) collective-permute-start(f32[34,8,128]{2,1,0:T(8,128)S(1)} %copy-done.19), channel_id=1, source_target_pairs={{0,24},{1,25},{8,16},{9,17},{16,8},{17,9},{24,0},{25,1},{2,26},{3,... | collective-permute-start | bytes 417800 | tf_op jit(solution)/shard_map/ppermute | solution.py:443
  23.7 10.6 %collective-permute-start.2 = (f32[2,32,8,128]{3,2,1,0:T(8,128)}, f32[2,32,8,128]{3,2,1,0:T(8,128)S(1)}, u32[]{:S(2)}, u32[]{:S(2)}) collective-permute-start(f32[2,32,8,128]{3,2,1,0:T(8,128)} %get-tuple-element.38), channel_id=1, source_target_pairs={{0,9},{1,8},{8,1},{9,0},{16,25},{17,24},{24,17},{25,16},{2,11},{3,... | collective-permute-start | bytes 786440 | tf_op jit(solution)/shard_map/ppermute | solution.py:443
  27.0 19.9 %collective-permute-start.3 = (f32[2,32,8,128]{3,2,1,0:T(8,128)}, f32[2,32,8,128]{3,2,1,0:T(8,128)S(1)}, u32[]{:S(2)}, u32[]{:S(2)}) collective-permute-start(f32[2,32,8,128]{3,2,1,0:T(8,128)} %get-tuple-element.39), channel_id=1, source_target_pairs={{0,16},{1,17},{8,24},{9,25},{16,0},{17,1},{24,8},{25,9},{2,18},{3,... | collective-permute-start | bytes 786440 | tf_op jit(solution)/shard_map/ppermute | solution.py:443
  28.4 18.6 %collective-permute-start.4 = (f32[2,32,8,128]{3,2,1,0:T(8,128)}, f32[2,32,8,128]{3,2,1,0:T(8,128)S(1)}, u32[]{:S(2)}, u32[]{:S(2)}) collective-permute-start(f32[2,32,8,128]{3,2,1,0:T(8,128)} %get-tuple-element.40), channel_id=1, source_target_pairs={{0,17},{1,16},{8,25},{9,24},{16,1},{17,0},{24,9},{25,8},{2,19},{3,... | collective-permute-start | bytes 786440 | tf_op jit(solution)/shard_map/ppermute | solution.py:443
  30.9 20.1 %collective-permute-start.5 = (f32[2,32,8,128]{3,2,1,0:T(8,128)}, f32[2,32,8,128]{3,2,1,0:T(8,128)S(1)}, u32[]{:S(2)}, u32[]{:S(2)}) collective-permute-start(f32[2,32,8,128]{3,2,1,0:T(8,128)} %get-tuple-element.41), channel_id=1, source_target_pairs={{0,24},{1,25},{8,16},{9,17},{16,8},{17,9},{24,0},{25,1},{2,26},{3,... | collective-permute-start | bytes 786440 | tf_op jit(solution)/shard_map/ppermute | solution.py:443
  32.8 19.5 %collective-permute-start.6 = (f32[2,32,8,128]{3,2,1,0:T(8,128)}, f32[2,32,8,128]{3,2,1,0:T(8,128)S(1)}, u32[]{:S(2)}, u32[]{:S(2)}) collective-permute-start(f32[2,32,8,128]{3,2,1,0:T(8,128)} %get-tuple-element.42), channel_id=1, source_target_pairs={{0,25},{1,24},{8,17},{9,16},{16,9},{17,8},{24,1},{25,0},{2,27},{3,... | collective-permute-start | bytes 786440 | tf_op jit(solution)/shard_map/ppermute | solution.py:443
  34.2 57.3 %copy-start.8 = (bf16[16,96]{1,0:T(8,128)(2,1)S(1)}, bf16[16,96]{1,0:T(8,128)(2,1)}, u32[]{:S(2)}) copy-start(bf16[16,96]{1,0:T(8,128)(2,1)} %constant.26.clone.refs_8_) | copy-start | bytes 9220
  34.3 20.1 %collective-permute-start.16 = (f32[34,8,128]{2,1,0:T(8,128)S(1)}, f32[34,8,128]{2,1,0:T(8,128)S(1)}, u32[]{:S(2)}, u32[]{:S(2)}) collective-permute-start(f32[34,8,128]{2,1,0:T(8,128)S(1)} %copy-done.18), channel_id=1, source_target_pairs={{0,1},{1,0},{8,9},{9,8},{16,17},{17,16},{24,25},{25,24},{2,3},{3,2... | collective-permute-start | bytes 417800 | tf_op jit(solution)/shard_map/ppermute | solution.py:443
  47.0 9.0 %collective-permute-start.17 = (f32[34,8,128]{2,1,0:T(8,128)S(1)}, f32[34,8,128]{2,1,0:T(8,128)S(1)}, u32[]{:S(2)}, u32[]{:S(2)}) collective-permute-start(f32[34,8,128]{2,1,0:T(8,128)S(1)} %copy-done.17), channel_id=1, source_target_pairs={{0,8},{1,9},{8,0},{9,1},{16,24},{17,25},{24,16},{25,17},{2,10},{3,... | collective-permute-start | bytes 417800 | tf_op jit(solution)/shard_map/ppermute | solution.py:443
  47.0 12.5 %collective-permute-start.18 = (f32[34,8,128]{2,1,0:T(8,128)S(1)}, f32[34,8,128]{2,1,0:T(8,128)S(1)}, u32[]{:S(2)}, u32[]{:S(2)}) collective-permute-start(f32[34,8,128]{2,1,0:T(8,128)S(1)} %copy-done.16), channel_id=1, source_target_pairs={{0,9},{1,8},{8,1},{9,0},{16,25},{17,24},{24,17},{25,16},{2,11},{3,... | collective-permute-start | bytes 417800 | tf_op jit(solution)/shard_map/ppermute | solution.py:443
  51.0 9.9 %collective-permute-start.19 = (f32[34,8,128]{2,1,0:T(8,128)S(1)}, f32[34,8,128]{2,1,0:T(8,128)S(1)}, u32[]{:S(2)}, u32[]{:S(2)}) collective-permute-start(f32[34,8,128]{2,1,0:T(8,128)S(1)} %copy-done.15), channel_id=1, source_target_pairs={{0,16},{1,17},{8,24},{9,25},{16,0},{17,1},{24,8},{25,9},{2,18},{3,... | collective-permute-start | bytes 417800 | tf_op jit(solution)/shard_map/ppermute | solution.py:443
  52.3 10.1 %collective-permute-start.20 = (f32[34,8,128]{2,1,0:T(8,128)S(1)}, f32[34,8,128]{2,1,0:T(8,128)S(1)}, u32[]{:S(2)}, u32[]{:S(2)}) collective-permute-start(f32[34,8,128]{2,1,0:T(8,128)S(1)} %copy-done.14), channel_id=1, source_target_pairs={{0,17},{1,16},{8,25},{9,24},{16,1},{17,0},{24,9},{25,8},{2,19},{3,... | collective-permute-start | bytes 417800 | tf_op jit(solution)/shard_map/ppermute | solution.py:443
  54.4 11.5 %collective-permute-start.21 = (f32[34,8,128]{2,1,0:T(8,128)S(1)}, f32[34,8,128]{2,1,0:T(8,128)S(1)}, u32[]{:S(2)}, u32[]{:S(2)}) collective-permute-start(f32[34,8,128]{2,1,0:T(8,128)S(1)} %copy-done.13), channel_id=1, source_target_pairs={{0,24},{1,25},{8,16},{9,17},{16,8},{17,9},{24,0},{25,1},{2,26},{3,... | collective-permute-start | bytes 417800 | tf_op jit(solution)/shard_map/ppermute | solution.py:443
  55.9 16.5 %collective-permute-start.24 = (f32[4,34,8,128]{3,2,1,0:T(8,128)S(1)}, f32[4,34,8,128]{3,2,1,0:T(8,128)S(1)}, u32[]{:S(2)}, u32[]{:S(2)}) collective-permute-start(f32[4,34,8,128]{3,2,1,0:T(8,128)S(1)} %pad_maximum_fusion.1), channel_id=1, source_target_pairs={{0,2},{2,4},{3,1},{4,6},{5,3},{7,5},{8,10},{10,12},{11,9},{12,14},... | collective-permute-start | bytes 1671176 | tf_op jit(solution)/shard_map/ppermute | solution.py:467
  59.5 17.4 %collective-permute-start.23 = (f32[4,34,8,128]{3,2,1,0:T(8,128)S(1)}, f32[4,34,8,128]{3,2,1,0:T(8,128)S(1)}, u32[]{:S(2)}, u32[]{:S(2)}) collective-permute-start(f32[4,34,8,128]{3,2,1,0:T(8,128)S(1)} %pad_maximum_fusion), channel_id=1, source_target_pairs={{1,3},{2,0},{3,5},{4,2},{5,7},{6,4},{9,11},{10,8},{11,13},{12,10},... | collective-permute-start | bytes 1671176 | tf_op jit(solution)/shard_map/ppermute | solution.py:467
  60.9 7.0 %collective-permute-start.22 = (f32[34,8,128]{2,1,0:T(8,128)S(1)}, f32[34,8,128]{2,1,0:T(8,128)S(1)}, u32[]{:S(2)}, u32[]{:S(2)}) collective-permute-start(f32[34,8,128]{2,1,0:T(8,128)S(1)} %copy-done.12), channel_id=1, source_target_pairs={{0,25},{1,24},{8,17},{9,16},{16,9},{17,8},{24,1},{25,0},{2,27},{3,... | collective-permute-start | bytes 417800 | tf_op jit(solution)/shard_map/ppermute | solution.py:443
  62.4 33.2 %collective-permute-start.8 = (f32[4,32,4,128]{3,2,1,0:T(4,128)S(1)}, f32[4,32,4,128]{3,2,1,0:T(4,128)S(1)}, u32[]{:S(2)}, u32[]{:S(2)}) collective-permute-start(f32[4,32,4,128]{3,2,1,0:T(4,128)S(1)} %pad_maximum_fusion.3), channel_id=1, source_target_pairs={{0,2},{2,4},{3,1},{4,6},{5,3},{7,5},{8,10},{10,12},{11,9},{12,14},... | collective-permute-start | bytes 786440 | tf_op jit(solution)/shard_map/ppermute | solution.py:467
  65.9 29.7 %collective-permute-start.7 = (f32[4,32,4,128]{3,2,1,0:T(4,128)S(1)}, f32[4,32,4,128]{3,2,1,0:T(4,128)S(1)}, u32[]{:S(2)}, u32[]{:S(2)}) collective-permute-start(f32[4,32,4,128]{3,2,1,0:T(4,128)S(1)} %pad_maximum_fusion.2), channel_id=1, source_target_pairs={{1,3},{2,0},{3,5},{4,2},{5,7},{6,4},{9,11},{10,8},{11,13},{12,10},... | collective-permute-start | bytes 786440 | tf_op jit(solution)/shard_map/ppermute | solution.py:467
  100.3 4.0 %collective-permute-start.25 = (f32[4,16,128]{2,1,0:T(8,128)S(1)}, f32[4,16,128]{2,1,0:T(8,128)S(1)}, u32[]{:S(2)}, u32[]{:S(2)}) collective-permute-start(f32[4,16,128]{2,1,0:T(8,128)S(1)} %get-tuple-element.61), channel_id=1, source_target_pairs={{0,1},{1,0},{2,3},{3,2},{4,5},{5,4},{6,7},{7,6},{8,9},{9,8},{10,11... | collective-permute-start | bytes 98312 | tf_op jit(solution)/shard_map/ppermute | solution.py:575
  (16 other events, 587.9 us)

commit v2 on v1

--- a/solution.py
+++ b/solution.py
@@ -256,9 +256,9 @@
 
 def first_kernel(groups, slab, extra, blocks, count_strips, factor, *refs):
     own, halos, refs = refs[: 2 * blocks], refs[2 * blocks : 2 * blocks + 2], refs[2 * blocks + 2 :]
-    lhs_ref, yw_ref, zh_ref, zl_ref, pair_ref, pal_ref = refs[:6]
-    outs = refs[6:-9]
-    zin, ein, sm, gx, gy, es, found_ref, fraction_ref, sems = refs[-9:]
+    lhs_ref, yw_ref, zh_ref, zl_ref, bins_ref, colour_ref, opacity_ref = refs[:7]
+    outs = refs[7:-11]
+    zin, ein, sm, gx, gy, es, found_ref, fraction_ref, pair_ref, pal_ref, sems = refs[-11:]
     copies = gather_rows(groups, slab, extra, own, halos, zin, ein, sems)
     planes = zin.shape[0] - 2 * RAD
     rows = sm.shape[1]
@@ -269,6 +269,19 @@
     clear_ends(zin, RAD)
     clear_ends(sm, RAD)
     clear_ends(ein, 1)
+
+    halves = bins_ref.shape[0]
+    lane = lax.broadcasted_iota(jnp.int32, (8, LANES), 1)
+    held = [jnp.broadcast_to(bins_ref[h : h + 1], (8, LANES)) for h in range(halves)]
+    moved = [pltpu.roll(value, LANES - 1, 1) for value in held]
+    for h in range(halves):
+        following = jnp.where(lane == LANES - 1, moved[min(h + 1, halves - 1)], moved[h])
+        pair_ref[h] = held[h] + LANES * following
+    pal_ref[...] = jnp.zeros(pal_ref.shape, jnp.float32)
+    colours_held = colour_ref.shape[1]
+    for c in range(3):
+        pal_ref[c, :, :colours_held] = jnp.broadcast_to(colour_ref[c : c + 1], (8, colours_held))
+    pal_ref[3, :, :colours_held] = jnp.broadcast_to(opacity_ref[...] * factor, (8, colours_held))
     for copy in copies:
         copy.wait()
     step = 8
@@ -311,13 +324,12 @@
         out = out[:, :LANES] + out[:, LANES:] + mxu(lo, yw_ref[:, :LANES])
         gy[pl.ds(start, step)] = out.reshape(step, rows, LANES)
 
-    halves = pair_ref.shape[0]
     bins = halves * LANES
     half = 0.5 * (bins - 1)
 
     def index_stage(t):
         start = pl.multiple_of(t * step, step)
-        pairs = [jnp.broadcast_to(pair_ref[h], (8, LANES)) for h in range(halves)]
+        pairs = [pair_ref[h] for h in range(halves)]
         for row in range(0, rows, 8):
             level = half * jnp.tanh(0.75 * sm[pl.ds(RAD + start, step), row : row + 8, :]) + half
             index = jnp.minimum(level.astype(jnp.int32), bins - 2)
@@ -332,7 +344,7 @@
 
     def colour_stage(t):
         start = pl.multiple_of(t * step, step)
-        colours = [jnp.broadcast_to(pal_ref[c], (8, LANES)) for c in range(4)]
+        colours = [pal_ref[c] for c in range(4)]
         for row in range(0, rows, 8):
             if row == 0 or row == rows - 8:
                 o_ref, at = outs[0], min(row, 8)
@@ -346,13 +358,19 @@
             grad_z = slope(sm[pl.ds(start, step + 2 * RAD), row : row + 8, :], step)
             grad_x = gx[pl.ds(start, step), row : row + 8, :]
             grad_y = gy[pl.ds(start, step), row : row + 8, :]
-            facing = jnp.abs(0.26726 * grad_z + 0.53452 * grad_x + 0.80178 * grad_y)
+            facing = jnp.abs(
+                (0.7 * 0.26726) * grad_z + (0.7 * 0.53452) * grad_x + (0.7 * 0.80178) * grad_y
+            )
             square = jnp.maximum(grad_z * grad_z + grad_x * grad_x + grad_y * grad_y, 0.1)
-            shade = 0.3 + 0.7 * facing * lax.rsqrt(square)
+            shade = 0.3 + facing * lax.rsqrt(square)
+            upper = shade * fraction
+            lower = shade - upper
             for i in range(step):
-                for c in range(4):
-                    looked = first[i][c] + fraction[i] * (second[i][c] - first[i][c])
-                    o_ref[c, start + i, at : at + 8, :] = looked * (shade[i] if c < 3 else factor)
+                for c in range(3):
+                    o_ref[c, start + i, at : at + 8, :] = first[i][c] * lower[i] + second[i][c] * upper[i]
+                o_ref[3, start + i, at : at + 8, :] = first[i][3] + fraction[i] * (
+                    second[i][3] - first[i][3]
+                )
 
     steps = planes // step
     smooth_stage(0)
@@ -374,16 +392,35 @@
     colour_stage(steps - 1)
 
 
-def second_kernel(groups, slab, blocks, haloed, joins, *refs):
+def composite(smooth, c_ref, start, carry):
+    through, red, green, blue = carry
+    for i in range(len(smooth)):
+        sigmoid = 0.5 * jnp.tanh(smooth[i]) + 0.5
+        passed = through * jnp.exp(-(c_ref[3, start + i] * sigmoid))
+        weight = through - passed
+        red = red + weight * c_ref[0, start + i]
+        green = green + weight * c_ref[1, start + i]
+        blue = blue + weight * c_ref[2, start + i]
+        through = passed
+    return through, red, green, blue
+
+
+def marched(step_of, planes, rows):
+    zero = jnp.zeros((rows, LANES), jnp.float32)
+    through, red, green, blue = lax.fori_loop(
+        0, planes // 8, step_of, (zero + 1.0, zero, zero, zero)
+    )
+    return red, green, blue, through
+
+
+def second_kernel(groups, slab, blocks, haloed, *refs):
     own, refs = refs[:blocks], refs[blocks:]
     halos, refs = (refs[:2], refs[2:]) if haloed else ((), refs)
-    (lhs_ref, c_ref), (zin, sm, sems) = refs[:2], refs[-3:]
-    image_ref, outs = (refs[2], refs[3:-3]) if joins else (None, refs[2:-3])
+    (lhs_ref, c_ref), outs, (zin, sm, sems) = refs[:2], refs[2:-3], refs[-3:]
     copies = gather_rows(groups, slab, 0, own, halos, zin, None, sems)
     planes = zin.shape[0] - 2 * RAD
-    rows = sm.shape[1]
+    rows = outs[0].shape[1]
     step = 8
-
     clear_ends(zin, RAD)
     for copy in copies:
         copy.wait()
@@ -393,34 +430,52 @@
         stack = plane_smooth(zin, start, step)
         for q in range(0, step, 2):
             out = mxu(lhs_ref[...], jnp.concatenate([stack[q], stack[q + 1]], axis=1))
-            sm[q] = out[:, :LANES]
-            sm[q + 1] = out[:, LANES:]
-        through, red, green, blue = carry
-        for i in range(step):
-            sigmoid = 0.5 * jnp.tanh(sm[i]) + 0.5
-            passed = through * jnp.exp(-(c_ref[3, start + i] * sigmoid))
-            weight = through - passed
-            red = red + weight * c_ref[0, start + i]
-            green = green + weight * c_ref[1, start + i]
-            blue = blue + weight * c_ref[2, start + i]
-            through = passed
-        return through, red, green, blue
-
-    zero = jnp.zeros((rows, LANES), jnp.float32)
-    through, red, green, blue = lax.fori_loop(
-        0, planes // step, march, (zero + 1.0, zero, zero, zero)
-    )
-    first = lax.rem(lax.axis_index(GROUP), groups) == 0
-    for c, value in enumerate((red, green, blue, through)):
-        if joins:
-            strips = (
-                jnp.concatenate([value[:8], image_ref[c, :8]], axis=0),
-                jnp.concatenate([image_ref[c, 8:], value[8:]], axis=0),
-            )
-            outs[0][c] = jnp.where(first, strips[0], strips[1])
-            outs[1][c] = jnp.where(first, strips[1], strips[0])
-        else:
-            outs[0][c] = value
+            for h in range(2):
+                part = out[:, h * LANES : (h + 1) * LANES]
+                sm[q + h] = part[:rows]
+                if len(outs) > 1:
+                    outs[1][start + q + h] = part[rows:]
+        return composite([sm[i] for i in range(step)], c_ref, start, carry)
+
+    for c, value in enumerate(marched(march, planes, rows)):
+        outs[0][c] = value
+
+
+def edge_kernel(groups, slab, one_ref, other_ref, lhs_ref, c_ref, part_ref, image_ref, *refs):
+    kept_ref, sent_ref, zin = refs
+    planes = zin.shape[0] - 2 * RAD
+    me = lax.axis_index(GROUP)
+    leads = lax.rem(me, groups) == groups - 1
+    clear_ends(zin, RAD)
+    for i in range(one_ref.shape[0]):
+        one, other = one_ref[i], other_ref[i]
+        zin[pl.ds(RAD + ((me // groups) ^ i) * slab, slab)] = jnp.concatenate(
+            [jnp.where(leads, one, other), jnp.where(leads, other, one)], axis=1
+        )
+    rows = part_ref.shape[1]
+    step = 8
+
+    def march(t, carry):
+        start = pl.multiple_of(t * step, step)
+        sums = symmetric(zin[pl.ds(start, step + 2 * RAD)], step)
+        hi, lo = split(sums)
+        hi, lo = hi.astype(jnp.float32), lo.astype(jnp.float32)
+        stack = jnp.concatenate([hi, lo, hi, jnp.zeros_like(hi)], axis=1).astype(jnp.bfloat16)
+        smooth = []
+        for q in range(0, step, 2):
+            out = mxu(lhs_ref[...], jnp.concatenate([stack[q], stack[q + 1]], axis=1))
+            smooth.append(part_ref[start + q] + out[:, :LANES])
+            smooth.append(part_ref[start + q + 1] + out[:, LANES:])
+        return composite(smooth, c_ref, start, carry)
+
+    first = lax.rem(me, groups) == 0
+    for c, value in enumerate(marched(march, planes, rows)):
+        strips = (
+            jnp.concatenate([value[:8], image_ref[c, :8]], axis=0),
+            jnp.concatenate([image_ref[c, 8:], value[8:]], axis=0),
+        )
+        kept_ref[c] = jnp.where(first, strips[0], strips[1])
+        sent_ref[c] = jnp.where(first, strips[1], strips[0])
 
 
 def vmem_call(kernel, shapes, scratch, in_specs, microseconds, limit):
@@ -497,7 +552,9 @@
         smooth, gradient = smooth_rows[RAD:-RAD], slope_rows @ (inside * smooth_rows)
         forms.append(three_terms(np.concatenate([smooth, gradient], axis=0)))
     edge_form = three_terms(smooth[outer])
-    inner_form = three_terms(smooth[inner][:, HALO:-HALO])
+    own_form = three_terms(np.concatenate([smooth[inner], smooth[outer]], axis=0)[:, HALO:-HALO])
+    near = np.r_[HALO - RAD : HALO, HALO + rows : HALO + rows + RAD]
+    near_form = np.pad(three_terms(smooth[outer][:, near]), ((0, 0), (0, 2 * RAD)))
     form = jnp.asarray(np.stack(forms))
     across = np.zeros((2 * LANES, LANES))
     across[:LANES] = band(D_TAPS, LANES, LANES, 0).T
@@ -510,10 +567,8 @@
     yw = np.concatenate(split_np(across), axis=1)
     zh, zl = split_np(np.kron(band(S_TAPS, PER, 3 * PER, PER).T, np.eye(2 * RAD)))
 
-    following = jnp.concatenate([tf_index[1:], tf_index[-1:]])
-    pair = (tf_index + LANES * following).reshape(bins // LANES, 1, LANES)
-    palette = jnp.concatenate([colour_palette, opacity_palette[None]], axis=0)
-    palette = jnp.pad(palette, ((0, 0), (0, LANES - palette.shape[1])))[:, None, :]
+    bin_rows = tf_index.reshape(bins // LANES, LANES)
+    opacity_row = opacity_palette.reshape(1, -1)
 
     anywhere = pl.BlockSpec(memory_space=pl.ANY)
     vmem = pl.BlockSpec(memory_space=pltpu.VMEM)
@@ -535,27 +590,39 @@
                 pltpu.VMEM((planes // PER, rows, LANES), f32),
                 pltpu.VMEM((2, 8, rows, LANES), jnp.int32),
                 pltpu.VMEM((2, 8, rows, LANES), f32),
+                pltpu.VMEM((bins // LANES, 8, LANES), jnp.int32),
+                pltpu.VMEM((4, 8, LANES), f32),
                 pltpu.SemaphoreType.DMA((4 * (blocks + depth),)),
             ],
-            [anywhere] * (2 * blocks + 2) + [vmem] * 6,
+            [anywhere] * (2 * blocks + 2) + [vmem] * 7,
             20,
             16,
-        )(*own, *halos, lhs, yw, zh, zl, pair, palette)
-
-    def march(own, halos, lhs, coloured, *others):
+        )(*own, *halos, lhs, yw, zh, zl, bin_rows, colour_palette, opacity_row)
+
+    def march(own, halos, lhs, coloured):
         mine, out = (wide, len(outer)) if halos else (rows, rows - len(outer))
         return vmem_call(
-            functools.partial(second_kernel, groups, slab, blocks, bool(halos), bool(others)),
-            [(4, out, LANES)] * (1 + len(others)),
+            functools.partial(second_kernel, groups, slab, blocks, bool(halos)),
+            [(4, out, LANES)] + ([] if halos else [(planes, rows - out, LANES)]),
             [
                 pltpu.VMEM((planes + 2 * RAD, mine, LANES), f32),
                 pltpu.VMEM((8, out, LANES), f32),
                 pltpu.SemaphoreType.DMA((2 * blocks,)),
             ],
-            [anywhere] * blocks + [vmem] * (len(halos) + 2 + len(others)),
+            [anywhere] * blocks + [vmem] * (len(halos) + 2),
             5,
             10,
-        )(*own, *halos, lhs, coloured, *others)
+        )(*own, *halos, lhs, coloured)
+
+    def edges(halos, coloured, sums, image):
+        return vmem_call(
+            functools.partial(edge_kernel, groups, slab),
+            [(4, strip, LANES)] * 2,
+            [pltpu.VMEM((planes + 2 * RAD, 2 * RAD, LANES), f32)],
+            [vmem] * 6,
+            3,
+            10,
+        )(*halos, near_form, coloured, sums, image)
 
     order = sorted(range(1, blocks), key=lambda m: (bin(m).count("1"), m))
     sent0 = list(source(fields, 0, groups, bands, True, False, 60 << 20))
@@ -566,12 +633,10 @@
     got1 = exchange(sent1, order)
     halo1 = row_halo(got1, groups, count, leads)
     coloured = colours(got0, halo0, form)
-    others = ()
-    if rows > len(outer):
-        others = march(got1, (), inner_form, coloured[1])
-    image = march(got1, halo1, edge_form, coloured[0], *others)
     if groups == 1:
-        return image[0]
+        return march(got1, halo1, edge_form, coloured[0])[0]
+    image, sums = march(got1, (), own_form, coloured[1])
+    image = edges(halo1, coloured[0], sums, image)
     given = lax.ppermute(image[1], "pair", [(0, 1), (1, 0)])
     return jnp.concatenate(
         [jnp.where(leads, given, image[0]), jnp.where(leads, image[0], given)], axis=2

time: 105 us -> 109 us (1.038)
  starting transfers between devices: 34.6 us -> 39.7 us
  waiting for transfers between devices: 31.2 us -> 33.3 us
  Pallas kernels: 34.6 us -> 33 us
    ppermute x21, waiting for transfers between devices: 18.4 us -> 31.4 us  [exchange(): got[m] = lax.ppermute(blocks[m], GROUP, pairs)]
    ppermute x4, waiting for transfers between devices: 8.91 us -> 0.01 us  [row_halo(): found.append(lax.ppermute(jnp.stack(edge), ('strips', 'pair'), pairs))]
    pallas_call x2 -> x1, Pallas kernels: 8.67 us -> 4.17 us  [march(): vmem_call(functools.partial(second_kernel, groups, slab, blocks, bool(hal...]
    pallas_call x0 -> x1, Pallas kernels: none -> 2.99 us  [edges(): vmem_call(functools.partial(edge_kernel, groups, slab), [(4, strip, LANES...]
    ppermute x1, starting transfers between devices: 0.07 us -> 2.63 us  [local(): given = lax.ppermute(image[1], 'pair', [(0, 1), (1, 0)])]
    ppermute x1, waiting for transfers between devices: 3.9 us -> 1.89 us  [local(): given = lax.ppermute(image[1], 'pair', [(0, 1), (1, 0)])]
    ppermute x21, starting transfers between devices: 24.9 us -> 26.6 us  [exchange(): got[m] = lax.ppermute(blocks[m], GROUP, pairs)]
  transfers between devices with their start and end apart: 26 -> 26, of which waited for: 9 -> 12; matrix products, arithmetic and copies ran while one was open for 3% -> 2% of each run, Pallas kernels for 23% -> 22%
where the time goes in v2:
time: 109 us
  starting transfers between devices  39.7 us (36%)
  waiting for transfers between devices  33.3 us (31%)
  Pallas kernels  33 us (30%)
  other arithmetic  2.65 us (2%)
    ppermute x21, waiting for transfers between devices, exchange(): got[m] = lax.ppermute(blocks[m], GROUP, pairs)  31.4 us
    ppermute x21, starting transfers between devices, exchange(): got[m] = lax.ppermute(blocks[m], GROUP, pairs)  26.6 us
    pallas_call x1, Pallas kernels, colours(): vmem_call(functools.partial(first_kernel, groups, slab, extra, blocks, co...  14.5 us
    pallas_call x2, Pallas kernels, source(): pl.pallas_call(functools.partial(source_kernel, blocks, groups, which, ex...  11.3 us
    ppermute x4, starting transfers between devices, row_halo(): found.append(lax.ppermute(jnp.stack(edge), ('strips', 'pair'), pairs))  10.5 us
    pallas_call x1, Pallas kernels, march(): vmem_call(functools.partial(second_kernel, groups, slab, blocks, bool(hal...  4.17 us
    pallas_call x1, Pallas kernels, edges(): vmem_call(functools.partial(edge_kernel, groups, slab), [(4, strip, LANES...  2.99 us
    ppermute x1, starting transfers between devices, local(): given = lax.ppermute(image[1], 'pair', [(0, 1), (1, 0)])  2.63 us
  transfers between devices with their start and end apart: 26, of which 12 were waited for; matrix products, arithmetic and copies ran while one was open for 2% of the time, Pallas kernels for 22%

profile of v2, /device:TPU:0, one launch (start us, length us, event | category | flops | bytes accessed | tf_op | source)
XLA Modules:
  0.0 109.2 jit_solution(2856067281357070158)
XLA Ops:
  0.0 6.2 %columns_filter.2 = (f32[34,8,128]{2,1,0:T(8,128)}, f32[34,8,128]{2,1,0:T(8,128)}, f32[34,8,128]{2,1,0:T(8,128)}, f32[34,8,128]{2,1,0:T(8,128)}, f32[34,8,128]{2...) custom-call(f32[2,32,16,1024]{3,2,1,0:T(8,128)} %refs_0_.3, ...), custom_call_target="tpu_custom_call" | custom-call | bytes 15000000 | tf_op jit(solution)/shard_map/columns_filter/pallas_call | solution.py:168
  6.3 3.0 %collective-permute-start.9 = (f32[34,8,128]{2,1,0:T(8,128)}, f32[34,8,128]{2,1,0:T(8,128)S(1)}, u32[]{:S(2)}, u32[]{:S(2)}) collective-permute-start(f32[34,8,128]{2,1,0:T(8,128)} %get-tuple-element.46), channel_id=1, source_target_pairs={{0,1},{1,0},{8,9},{9,8},{16,17},{17,16},{24,25},{25,24},{2,3},{3,2... | collective-permute-start | bytes 417800 | tf_op jit(solution)/shard_map/ppermute | solution.py:498
  9.3 2.1 %collective-permute-start.13 = (f32[34,8,128]{2,1,0:T(8,128)}, f32[34,8,128]{2,1,0:T(8,128)S(1)}, u32[]{:S(2)}, u32[]{:S(2)}) collective-permute-start(f32[34,8,128]{2,1,0:T(8,128)} %get-tuple-element.50), channel_id=1, source_target_pairs={{0,17},{1,16},{8,25},{9,24},{16,1},{17,0},{24,9},{25,8},{2,19},{3,... | collective-permute-start | bytes 417800 | tf_op jit(solution)/shard_map/ppermute | solution.py:498
  12.2 5.2 %columns_filter.3 = (f32[2,32,8,128]{3,2,1,0:T(8,128)}, f32[2,32,8,128]{3,2,1,0:T(8,128)}, f32[2,32,8,128]{3,2,1,0:T(8,128)}, f32[2,32,8,128]{3,2,1,0:T(8,128)},...) custom-call(f32[2,32,16,1024]{3,2,1,0:T(8,128)} %refs_0_.3, ...), custom_call_target="tpu_custom_call" | custom-call | bytes 15000000 | tf_op jit(solution)/shard_map/columns_filter/pallas_call | solution.py:168
  17.8 1.5 %collective-permute-start.1 = (f32[2,32,8,128]{3,2,1,0:T(8,128)}, f32[2,32,8,128]{3,2,1,0:T(8,128)S(1)}, u32[]{:S(2)}, u32[]{:S(2)}) collective-permute-start(f32[2,32,8,128]{3,2,1,0:T(8,128)} %get-tuple-element.39), channel_id=1, source_target_pairs={{0,16},{1,17},{8,24},{9,25},{16,0},{17,1},{24,8},{25,9},{2,18},{3,... | collective-permute-start | bytes 786440 | tf_op jit(solution)/shard_map/ppermute | solution.py:498
  19.4 2.0 %collective-permute-done.13.refs_5_ = f32[34,8,128]{2,1,0:T(8,128)S(1)} collective-permute-done((f32[34,8,128]{2,1,0:T(8,128)}, f32[34,8,128]{2,1,0:T(8,128)S(1)}, u32[]{:S(2)}, u32[]{:S(2)}) %collective-permute-start.13) | collective-permute-done | bytes 139296 | tf_op jit(solution)/shard_map/ppermute | solution.py:498
  21.3 1.2 %collective-permute-done.15.refs_7_ = f32[34,8,128]{2,1,0:T(8,128)S(1)} collective-permute-done((f32[34,8,128]{2,1,0:T(8,128)}, f32[34,8,128]{2,1,0:T(8,128)S(1)}, u32[]{:S(2)}, u32[]{:S(2)}) %collective-permute-start.15) | collective-permute-done | bytes 139296 | tf_op jit(solution)/shard_map/ppermute | solution.py:498
  24.3 7.8 %collective-permute-done.12.refs_4_ = f32[34,8,128]{2,1,0:T(8,128)S(1)} collective-permute-done((f32[34,8,128]{2,1,0:T(8,128)S(1)}, f32[34,8,128]{2,1,0:T(8,128)S(1)}, u32[]{:S(2)}, u32[]{:S(2)}) %collective-permute-start.12) | collective-permute-done | bytes 139296 | tf_op jit(solution)/shard_map/ppermute | solution.py:498
  32.0 1.5 %collective-permute-start.4 = (f32[2,32,8,128]{3,2,1,0:T(8,128)}, f32[2,32,8,128]{3,2,1,0:T(8,128)S(1)}, u32[]{:S(2)}, u32[]{:S(2)}) collective-permute-start(f32[2,32,8,128]{3,2,1,0:T(8,128)} %get-tuple-element.41), channel_id=1, source_target_pairs={{0,1},{1,0},{8,9},{9,8},{16,17},{17,16},{24,25},{25,24},{2,3},{3,2... | collective-permute-start | bytes 786440 | tf_op jit(solution)/shard_map/ppermute | solution.py:498
  33.5 1.4 %collective-permute-done.14.refs_6_ = f32[34,8,128]{2,1,0:T(8,128)S(1)} collective-permute-done((f32[34,8,128]{2,1,0:T(8,128)S(1)}, f32[34,8,128]{2,1,0:T(8,128)S(1)}, u32[]{:S(2)}, u32[]{:S(2)}) %collective-permute-start.14) | collective-permute-done | bytes 139296 | tf_op jit(solution)/shard_map/ppermute | solution.py:498
  34.8 1.3 %collective-permute-start.5 = (f32[2,32,8,128]{3,2,1,0:T(8,128)}, f32[2,32,8,128]{3,2,1,0:T(8,128)S(1)}, u32[]{:S(2)}, u32[]{:S(2)}) collective-permute-start(f32[2,32,8,128]{3,2,1,0:T(8,128)} %get-tuple-element.42), channel_id=1, source_target_pairs={{0,9},{1,8},{8,1},{9,0},{16,25},{17,24},{24,17},{25,16},{2,11},{3,... | collective-permute-start | bytes 786440 | tf_op jit(solution)/shard_map/ppermute | solution.py:498
  36.4 2.3 %collective-permute-start.7 = (f32[2,32,8,128]{3,2,1,0:T(8,128)}, f32[2,32,8,128]{3,2,1,0:T(8,128)S(1)}, u32[]{:S(2)}, u32[]{:S(2)}) collective-permute-start(f32[2,32,8,128]{3,2,1,0:T(8,128)} %get-tuple-element.44), channel_id=1, source_target_pairs={{0,25},{1,24},{8,17},{9,16},{16,9},{17,8},{24,1},{25,0},{2,27},{3,... | collective-permute-start | bytes 786440 | tf_op jit(solution)/shard_map/ppermute | solution.py:498
  40.5 1.5 %collective-permute-start.16 = (f32[34,8,128]{2,1,0:T(8,128)S(1)}, f32[34,8,128]{2,1,0:T(8,128)S(1)}, u32[]{:S(2)}, u32[]{:S(2)}) collective-permute-start(f32[34,8,128]{2,1,0:T(8,128)S(1)} %copy-done.18), channel_id=1, source_target_pairs={{0,1},{1,0},{8,9},{9,8},{16,17},{17,16},{24,25},{25,24},{2,3},{3,2... | collective-permute-start | bytes 417800 | tf_op jit(solution)/shard_map/ppermute | solution.py:498
  42.0 4.1 %collective-permute-done.5.refs_3_ = f32[2,32,8,128]{3,2,1,0:T(8,128)S(1)} collective-permute-done((f32[2,32,8,128]{3,2,1,0:T(8,128)}, f32[2,32,8,128]{3,2,1,0:T(8,128)S(1)}, u32[]{:S(2)}, u32[]{:S(2)}) %collective-permute-start.5) | collective-permute-done | bytes 262176 | tf_op jit(solution)/shard_map/ppermute | solution.py:498
  46.1 2.1 %collective-permute-start.18 = (f32[34,8,128]{2,1,0:T(8,128)S(1)}, f32[34,8,128]{2,1,0:T(8,128)S(1)}, u32[]{:S(2)}, u32[]{:S(2)}) collective-permute-start(f32[34,8,128]{2,1,0:T(8,128)S(1)} %copy-done.16), channel_id=1, source_target_pairs={{0,9},{1,8},{8,1},{9,0},{16,25},{17,24},{24,17},{25,16},{2,11},{3,... | collective-permute-start | bytes 417800 | tf_op jit(solution)/shard_map/ppermute | solution.py:498
  48.2 4.1 %collective-permute-done.6.refs_5_ = f32[2,32,8,128]{3,2,1,0:T(8,128)S(1)} collective-permute-done((f32[2,32,8,128]{3,2,1,0:T(8,128)}, f32[2,32,8,128]{3,2,1,0:T(8,128)S(1)}, u32[]{:S(2)}, u32[]{:S(2)}) %collective-permute-start.6) | collective-permute-done | bytes 262176 | tf_op jit(solution)/shard_map/ppermute | solution.py:498
  52.3 3.7 %collective-permute-start.24 = (f32[4,34,8,128]{3,2,1,0:T(8,128)S(1)}, f32[4,34,8,128]{3,2,1,0:T(8,128)S(1)}, u32[]{:S(2)}, u32[]{:S(2)}) collective-permute-start(f32[4,34,8,128]{3,2,1,0:T(8,128)S(1)} %pad_maximum_fusion.1), channel_id=1, source_target_pairs={{0,2},{2,4},{3,1},{4,6},{5,3},{7,5},{8,10},{10,12},{11,9},{12,14},... | collective-permute-start | bytes 1671176 | tf_op jit(solution)/shard_map/ppermute | solution.py:522
  56.1 1.3 %collective-permute-done.7.refs_7_ = f32[2,32,8,128]{3,2,1,0:T(8,128)S(1)} collective-permute-done((f32[2,32,8,128]{3,2,1,0:T(8,128)}, f32[2,32,8,128]{3,2,1,0:T(8,128)S(1)}, u32[]{:S(2)}, u32[]{:S(2)}) %collective-permute-start.7) | collective-permute-done | bytes 262176 | tf_op jit(solution)/shard_map/ppermute | solution.py:498
  57.3 1.3 %collective-permute-start.23 = (f32[4,34,8,128]{3,2,1,0:T(8,128)S(1)}, f32[4,34,8,128]{3,2,1,0:T(8,128)S(1)}, u32[]{:S(2)}, u32[]{:S(2)}) collective-permute-start(f32[4,34,8,128]{3,2,1,0:T(8,128)S(1)} %pad_maximum_fusion), channel_id=1, source_target_pairs={{1,3},{2,0},{3,5},{4,2},{5,7},{6,4},{9,11},{10,8},{11,13},{12,10},... | collective-permute-start | bytes 1671176 | tf_op jit(solution)/shard_map/ppermute | solution.py:522
  59.7 1.5 %collective-permute-done.16.refs_9_ = f32[34,8,128]{2,1,0:T(8,128)S(1)} collective-permute-done((f32[34,8,128]{2,1,0:T(8,128)S(1)}, f32[34,8,128]{2,1,0:T(8,128)S(1)}, u32[]{:S(2)}, u32[]{:S(2)}) %collective-permute-start.16) | collective-permute-done | bytes 139296 | tf_op jit(solution)/shard_map/ppermute | solution.py:498
  61.5 2.7 %collective-permute-start.20 = (f32[34,8,128]{2,1,0:T(8,128)S(1)}, f32[34,8,128]{2,1,0:T(8,128)S(1)}, u32[]{:S(2)}, u32[]{:S(2)}) collective-permute-start(f32[34,8,128]{2,1,0:T(8,128)S(1)} %copy-done.14), channel_id=1, source_target_pairs={{0,17},{1,16},{8,25},{9,24},{16,1},{17,0},{24,9},{25,8},{2,19},{3,... | collective-permute-start | bytes 417800 | tf_op jit(solution)/shard_map/ppermute | solution.py:498
  64.3 1.8 %collective-permute-start.21 = (f32[34,8,128]{2,1,0:T(8,128)S(1)}, f32[34,8,128]{2,1,0:T(8,128)S(1)}, u32[]{:S(2)}, u32[]{:S(2)}) collective-permute-start(f32[34,8,128]{2,1,0:T(8,128)S(1)} %copy-done.13), channel_id=1, source_target_pairs={{0,24},{1,25},{8,16},{9,17},{16,8},{17,9},{24,0},{25,1},{2,26},{3,... | collective-permute-start | bytes 417800 | tf_op jit(solution)/shard_map/ppermute | solution.py:498
  66.2 3.4 %collective-permute-done.19.refs_12_ = f32[34,8,128]{2,1,0:T(8,128)S(1)} collective-permute-done((f32[34,8,128]{2,1,0:T(8,128)S(1)}, f32[34,8,128]{2,1,0:T(8,128)S(1)}, u32[]{:S(2)}, u32[]{:S(2)}) %collective-permute-start.19) | collective-permute-done | bytes 139296 | tf_op jit(solution)/shard_map/ppermute | solution.py:498
  69.5 4.2 %collective-permute-start.8 = (f32[4,32,4,128]{3,2,1,0:T(4,128)S(1)}, f32[4,32,4,128]{3,2,1,0:T(4,128)S(1)}, u32[]{:S(2)}, u32[]{:S(2)}) collective-permute-start(f32[4,32,4,128]{3,2,1,0:T(4,128)S(1)} %pad_maximum_fusion.3), channel_id=1, source_target_pairs={{0,2},{2,4},{3,1},{4,6},{5,3},{7,5},{8,10},{10,12},{11,9},{12,14},... | collective-permute-start | bytes 786440 | tf_op jit(solution)/shard_map/ppermute | solution.py:522
  73.7 1.3 %collective-permute-start.3 = (f32[4,32,4,128]{3,2,1,0:T(4,128)S(1)}, f32[4,32,4,128]{3,2,1,0:T(4,128)S(1)}, u32[]{:S(2)}, u32[]{:S(2)}) collective-permute-start(f32[4,32,4,128]{3,2,1,0:T(4,128)S(1)} %pad_maximum_fusion.2), channel_id=1, source_target_pairs={{1,3},{2,0},{3,5},{4,2},{5,7},{6,4},{9,11},{10,8},{11,13},{12,10},... | collective-permute-start | bytes 786440 | tf_op jit(solution)/shard_map/ppermute | solution.py:522
  75.0 3.3 %collective-permute-start.22 = (f32[34,8,128]{2,1,0:T(8,128)S(1)}, f32[34,8,128]{2,1,0:T(8,128)S(1)}, u32[]{:S(2)}, u32[]{:S(2)}) collective-permute-start(f32[34,8,128]{2,1,0:T(8,128)S(1)} %copy-done.12), channel_id=1, source_target_pairs={{0,25},{1,24},{8,17},{9,16},{16,9},{17,8},{24,1},{25,0},{2,27},{3,... | collective-permute-start | bytes 417800 | tf_op jit(solution)/shard_map/ppermute | solution.py:498
  78.4 3.8 %collective-permute-done.22.refs_15_ = f32[34,8,128]{2,1,0:T(8,128)S(1)} collective-permute-done((f32[34,8,128]{2,1,0:T(8,128)S(1)}, f32[34,8,128]{2,1,0:T(8,128)S(1)}, u32[]{:S(2)}, u32[]{:S(2)}) %collective-permute-start.22) | collective-permute-done | bytes 139296 | tf_op jit(solution)/shard_map/ppermute | solution.py:498
  82.3 14.5 %shard_map.109 = (f32[4,128,16,128]{3,2,1,0:T(8,128)S(1)}, f32[4,128,16,128]{3,2,1,0:T(8,128)S(1)}) custom-call(f32[34,8,128]{2,1,0:T(8,128)S(1)} %copy-done.1, f32[34,8,128]{2,1,0:T(8,128)S(1)} %collective-permute-done.9.refs_1_, f32[34,8,128]{2,1,0:T(8,128)S(1)} %collective-permute-done.10.refs_2_, f32[34,8,128]{2,1,0:T(8,128)S(1)} %collective-permute-done.11.refs_3_, ...), custom_call_target="tpu_custom_call" | custom-call | bytes 60000000 | tf_op jit(solution)/shard_map/pallas_call | solution.py:581
  96.8 4.2 %shard_map.110 = (f32[4,16,128]{2,1,0:T(8,128)S(1)}, f32[128,16,128]{2,1,0:T(8,128)S(1)}) custom-call(f32[2,32,8,128]{3,2,1,0:T(8,128)S(1)} %copy-done, f32[2,32,8,128]{3,2,1,0:T(8,128)S(1)} %collective-permute-done.4.refs_1_, f32[2,32,8,128]{3,2,1,0:T(8,128)S(1)} %collective-permute-done.refs_2_, f32[2,32,8,128]{3,2,1,0:T(8,128)S(1)} %collective-permute-done.5.refs_3_, ...), custom_call_target="tpu_custom_call" | custom-call | bytes 15000000 | tf_op jit(solution)/shard_map/pallas_call | solution.py:604
  101.0 3.0 %shard_map.111 = (f32[4,16,128]{2,1,0:T(8,128)S(1)}, f32[4,16,128]{2,1,0:T(8,128)S(1)}) custom-call(f32[4,32,4,128]{3,2,1,0:T(4,128)S(1)} %collective-permute-done.3.one_ref, f32[4,32,4,128]{3,2,1,0:T(4,128)S(1)} %collective-permute-done.8.other_ref, bf16[16,32]{1,0:T(8,128)(2,1)S(1)} %copy-done.8, f32[4,128,16,128]{3,2,1,0:T(8,128)S(1)} %get-tuple-element.61.c_ref, ...), custom_call_target="tpu_custom_call" | custom-call | bytes 9000000 | tf_op jit(solution)/shard_map/pallas_call | solution.py:618
  104.0 2.6 %collective-permute-start.25 = (f32[4,16,128]{2,1,0:T(8,128)S(1)}, f32[4,16,128]{2,1,0:T(8,128)S(1)}, u32[]{:S(2)}, u32[]{:S(2)}) collective-permute-start(f32[4,16,128]{2,1,0:T(8,128)S(1)} %get-tuple-element.65), channel_id=1, source_target_pairs={{0,1},{1,0},{2,3},{3,2},{4,5},{5,4},{6,7},{7,6},{8,9},{9,8},{10,11... | collective-permute-start | bytes 98312 | tf_op jit(solution)/shard_map/ppermute | solution.py:640
  106.6 1.9 %collective-permute-done.25 = f32[4,16,128]{2,1,0:T(8,128)S(1)} collective-permute-done((f32[4,16,128]{2,1,0:T(8,128)S(1)}, f32[4,16,128]{2,1,0:T(8,128)S(1)}, u32[]{:S(2)}, u32[]{:S(2)}) %collective-permute-start.25) | collective-permute-done | bytes 32800 | tf_op jit(solution)/shard_map/ppermute | solution.py:640
  (77 shorter events, 7.1 us)
Async XLA Ops:
  6.3 11.5 %collective-permute-start.9 = (f32[34,8,128]{2,1,0:T(8,128)}, f32[34,8,128]{2,1,0:T(8,128)S(1)}, u32[]{:S(2)}, u32[]{:S(2)}) collective-permute-start(f32[34,8,128]{2,1,0:T(8,128)} %get-tuple-element.46), channel_id=1, source_target_pairs={{0,1},{1,0},{8,9},{9,8},{16,17},{17,16},{24,25},{25,24},{2,3},{3,2... | collective-permute-start | bytes 417800 | tf_op jit(solution)/shard_map/ppermute | solution.py:498
  9.3 10.0 %collective-permute-start.11 = (f32[34,8,128]{2,1,0:T(8,128)}, f32[34,8,128]{2,1,0:T(8,128)S(1)}, u32[]{:S(2)}, u32[]{:S(2)}) collective-permute-start(f32[34,8,128]{2,1,0:T(8,128)} %get-tuple-element.48), channel_id=1, source_target_pairs={{0,9},{1,8},{8,1},{9,0},{16,25},{17,24},{24,17},{25,16},{2,11},{3,... | collective-permute-start | bytes 417800 | tf_op jit(solution)/shard_map/ppermute | solution.py:498
  9.3 12.0 %collective-permute-start.13 = (f32[34,8,128]{2,1,0:T(8,128)}, f32[34,8,128]{2,1,0:T(8,128)S(1)}, u32[]{:S(2)}, u32[]{:S(2)}) collective-permute-start(f32[34,8,128]{2,1,0:T(8,128)} %get-tuple-element.50), channel_id=1, source_target_pairs={{0,17},{1,16},{8,25},{9,24},{16,1},{17,0},{24,9},{25,8},{2,19},{3,... | collective-permute-start | bytes 417800 | tf_op jit(solution)/shard_map/ppermute | solution.py:498
  11.4 70.8 %copy-start.2 = (f32[34,8,128]{2,1,0:T(8,128)S(1)}, f32[34,8,128]{2,1,0:T(8,128)}, u32[]{:S(2)}) copy-start(f32[34,8,128]{2,1,0:T(8,128)} %get-tuple-element.53.refs_8_) | copy-start | bytes 417796
  11.5 70.8 %copy-start.3 = (bf16[4,64,144]{2,1,0:T(8,128)(2,1)S(1)}, bf16[4,64,144]{2,1,0:T(8,128)(2,1)}, u32[]{:S(2)}) copy-start(bf16[4,64,144]{2,1,0:T(8,128)(2,1)} %constant.17.clone.refs_18_) | copy-start | bytes 221188
  11.5 70.7 %copy-start.4 = (bf16[256,256]{1,0:T(8,128)(2,1)S(1)}, bf16[256,256]{1,0:T(8,128)(2,1)}, u32[]{:S(2)}) copy-start(bf16[256,256]{1,0:T(8,128)(2,1)} %constant.18.clone.refs_19_) | copy-start | bytes 393220
  11.5 70.7 %copy-start.5 = (bf16[384,128]{1,0:T(8,128)(2,1)S(1)}, bf16[384,128]{1,0:T(8,128)(2,1)}, u32[]{:S(2)}) copy-start(bf16[384,128]{1,0:T(8,128)(2,1)} %constant.19.clone.refs_20_) | copy-start | bytes 294916
  11.5 70.7 %copy-start.6 = (bf16[384,128]{1,0:T(8,128)(2,1)S(1)}, bf16[384,128]{1,0:T(8,128)(2,1)}, u32[]{:S(2)}) copy-start(bf16[384,128]{1,0:T(8,128)(2,1)} %constant.20.clone.refs_21_) | copy-start | bytes 294916
  11.5 70.7 %copy-start.9 = (f32[3,16]{1,0:T(4,128)S(1)}, f32[3,16]{1,0:T(4,128)}, u32[]{:S(2)}) copy-start(f32[3,16]{1,0:T(4,128)} %refs_23_.1) | copy-start | bytes 580
  11.5 11.0 %collective-permute-start.15 = (f32[34,8,128]{2,1,0:T(8,128)}, f32[34,8,128]{2,1,0:T(8,128)S(1)}, u32[]{:S(2)}, u32[]{:S(2)}) collective-permute-start(f32[34,8,128]{2,1,0:T(8,128)} %get-tuple-element.52), channel_id=1, source_target_pairs={{0,25},{1,24},{8,17},{9,16},{16,9},{17,8},{24,1},{25,0},{2,27},{3,... | collective-permute-start | bytes 417800 | tf_op jit(solution)/shard_map/ppermute | solution.py:498
  17.4 18.8 %collective-permute-start = (f32[2,32,8,128]{3,2,1,0:T(8,128)}, f32[2,32,8,128]{3,2,1,0:T(8,128)S(1)}, u32[]{:S(2)}, u32[]{:S(2)}) collective-permute-start(f32[2,32,8,128]{3,2,1,0:T(8,128)} %get-tuple-element.38), channel_id=1, source_target_pairs={{0,8},{1,9},{8,0},{9,1},{16,24},{17,25},{24,16},{25,17},{2,10},{3,... | collective-permute-start | bytes 786440 | tf_op jit(solution)/shard_map/ppermute | solution.py:498
  17.8 18.6 %collective-permute-start.1 = (f32[2,32,8,128]{3,2,1,0:T(8,128)}, f32[2,32,8,128]{3,2,1,0:T(8,128)S(1)}, u32[]{:S(2)}, u32[]{:S(2)}) collective-permute-start(f32[2,32,8,128]{3,2,1,0:T(8,128)} %get-tuple-element.39), channel_id=1, source_target_pairs={{0,16},{1,17},{8,24},{9,25},{16,0},{17,1},{24,8},{25,9},{2,18},{3,... | collective-permute-start | bytes 786440 | tf_op jit(solution)/shard_map/ppermute | solution.py:498
  19.3 3.8 %collective-permute-start.10 = (f32[34,8,128]{2,1,0:T(8,128)S(1)}, f32[34,8,128]{2,1,0:T(8,128)S(1)}, u32[]{:S(2)}, u32[]{:S(2)}) collective-permute-start(f32[34,8,128]{2,1,0:T(8,128)S(1)} %copy-done.21), channel_id=1, source_target_pairs={{0,8},{1,9},{8,0},{9,1},{16,24},{17,25},{24,16},{25,17},{2,10},{3,... | collective-permute-start | bytes 417800 | tf_op jit(solution)/shard_map/ppermute | solution.py:498
  21.3 10.7 %collective-permute-start.12 = (f32[34,8,128]{2,1,0:T(8,128)S(1)}, f32[34,8,128]{2,1,0:T(8,128)S(1)}, u32[]{:S(2)}, u32[]{:S(2)}) collective-permute-start(f32[34,8,128]{2,1,0:T(8,128)S(1)} %copy-done.20), channel_id=1, source_target_pairs={{0,16},{1,17},{8,24},{9,25},{16,0},{17,1},{24,8},{25,9},{2,18},{3,... | collective-permute-start | bytes 417800 | tf_op jit(solution)/shard_map/ppermute | solution.py:498
  22.5 12.3 %collective-permute-start.14 = (f32[34,8,128]{2,1,0:T(8,128)S(1)}, f32[34,8,128]{2,1,0:T(8,128)S(1)}, u32[]{:S(2)}, u32[]{:S(2)}) collective-permute-start(f32[34,8,128]{2,1,0:T(8,128)S(1)} %copy-done.19), channel_id=1, source_target_pairs={{0,24},{1,25},{8,16},{9,17},{16,8},{17,9},{24,0},{25,1},{2,26},{3,... | collective-permute-start | bytes 417800 | tf_op jit(solution)/shard_map/ppermute | solution.py:498
  23.1 17.3 %collective-permute-start.2 = (f32[2,32,8,128]{3,2,1,0:T(8,128)}, f32[2,32,8,128]{3,2,1,0:T(8,128)S(1)}, u32[]{:S(2)}, u32[]{:S(2)}) collective-permute-start(f32[2,32,8,128]{3,2,1,0:T(8,128)} %get-tuple-element.40), channel_id=1, source_target_pairs={{0,24},{1,25},{8,16},{9,17},{16,8},{17,9},{24,0},{25,1},{2,26},{3,... | collective-permute-start | bytes 786440 | tf_op jit(solution)/shard_map/ppermute | solution.py:498
  32.0 10.0 %collective-permute-start.4 = (f32[2,32,8,128]{3,2,1,0:T(8,128)}, f32[2,32,8,128]{3,2,1,0:T(8,128)S(1)}, u32[]{:S(2)}, u32[]{:S(2)}) collective-permute-start(f32[2,32,8,128]{3,2,1,0:T(8,128)} %get-tuple-element.41), channel_id=1, source_target_pairs={{0,1},{1,0},{8,9},{9,8},{16,17},{17,16},{24,25},{25,24},{2,3},{3,2... | collective-permute-start | bytes 786440 | tf_op jit(solution)/shard_map/ppermute | solution.py:498
  34.8 11.3 %collective-permute-start.5 = (f32[2,32,8,128]{3,2,1,0:T(8,128)}, f32[2,32,8,128]{3,2,1,0:T(8,128)S(1)}, u32[]{:S(2)}, u32[]{:S(2)}) collective-permute-start(f32[2,32,8,128]{3,2,1,0:T(8,128)} %get-tuple-element.42), channel_id=1, source_target_pairs={{0,9},{1,8},{8,1},{9,0},{16,25},{17,24},{24,17},{25,16},{2,11},{3,... | collective-permute-start | bytes 786440 | tf_op jit(solution)/shard_map/ppermute | solution.py:498
  36.2 16.1 %collective-permute-start.6 = (f32[2,32,8,128]{3,2,1,0:T(8,128)}, f32[2,32,8,128]{3,2,1,0:T(8,128)S(1)}, u32[]{:S(2)}, u32[]{:S(2)}) collective-permute-start(f32[2,32,8,128]{3,2,1,0:T(8,128)} %get-tuple-element.43), channel_id=1, source_target_pairs={{0,17},{1,16},{8,25},{9,24},{16,1},{17,0},{24,9},{25,8},{2,19},{3,... | collective-permute-start | bytes 786440 | tf_op jit(solution)/shard_map/ppermute | solution.py:498
  36.4 20.9 %collective-permute-start.7 = (f32[2,32,8,128]{3,2,1,0:T(8,128)}, f32[2,32,8,128]{3,2,1,0:T(8,128)S(1)}, u32[]{:S(2)}, u32[]{:S(2)}) collective-permute-start(f32[2,32,8,128]{3,2,1,0:T(8,128)} %get-tuple-element.44), channel_id=1, source_target_pairs={{0,25},{1,24},{8,17},{9,16},{16,9},{17,8},{24,1},{25,0},{2,27},{3,... | collective-permute-start | bytes 786440 | tf_op jit(solution)/shard_map/ppermute | solution.py:498
  40.5 20.8 %collective-permute-start.16 = (f32[34,8,128]{2,1,0:T(8,128)S(1)}, f32[34,8,128]{2,1,0:T(8,128)S(1)}, u32[]{:S(2)}, u32[]{:S(2)}) collective-permute-start(f32[34,8,128]{2,1,0:T(8,128)S(1)} %copy-done.18), channel_id=1, source_target_pairs={{0,1},{1,0},{8,9},{9,8},{16,17},{17,16},{24,25},{25,24},{2,3},{3,2... | collective-permute-start | bytes 417800 | tf_op jit(solution)/shard_map/ppermute | solution.py:498
  42.0 19.5 %collective-permute-start.17 = (f32[34,8,128]{2,1,0:T(8,128)S(1)}, f32[34,8,128]{2,1,0:T(8,128)S(1)}, u32[]{:S(2)}, u32[]{:S(2)}) collective-permute-start(f32[34,8,128]{2,1,0:T(8,128)S(1)} %copy-done.17), channel_id=1, source_target_pairs={{0,8},{1,9},{8,0},{9,1},{16,24},{17,25},{24,16},{25,17},{2,10},{3,... | collective-permute-start | bytes 417800 | tf_op jit(solution)/shard_map/ppermute | solution.py:498
  46.1 18.1 %collective-permute-start.18 = (f32[34,8,128]{2,1,0:T(8,128)S(1)}, f32[34,8,128]{2,1,0:T(8,128)S(1)}, u32[]{:S(2)}, u32[]{:S(2)}) collective-permute-start(f32[34,8,128]{2,1,0:T(8,128)S(1)} %copy-done.16), channel_id=1, source_target_pairs={{0,9},{1,8},{8,1},{9,0},{16,25},{17,24},{24,17},{25,16},{2,11},{3,... | collective-permute-start | bytes 417800 | tf_op jit(solution)/shard_map/ppermute | solution.py:498
  52.3 29.9 %collective-permute-start.24 = (f32[4,34,8,128]{3,2,1,0:T(8,128)S(1)}, f32[4,34,8,128]{3,2,1,0:T(8,128)S(1)}, u32[]{:S(2)}, u32[]{:S(2)}) collective-permute-start(f32[4,34,8,128]{3,2,1,0:T(8,128)S(1)} %pad_maximum_fusion.1), channel_id=1, source_target_pairs={{0,2},{2,4},{3,1},{4,6},{5,3},{7,5},{8,10},{10,12},{11,9},{12,14},... | collective-permute-start | bytes 1671176 | tf_op jit(solution)/shard_map/ppermute | solution.py:522
  57.3 24.9 %collective-permute-start.23 = (f32[4,34,8,128]{3,2,1,0:T(8,128)S(1)}, f32[4,34,8,128]{3,2,1,0:T(8,128)S(1)}, u32[]{:S(2)}, u32[]{:S(2)}) collective-permute-start(f32[4,34,8,128]{3,2,1,0:T(8,128)S(1)} %pad_maximum_fusion), channel_id=1, source_target_pairs={{1,3},{2,0},{3,5},{4,2},{5,7},{6,4},{9,11},{10,8},{11,13},{12,10},... | collective-permute-start | bytes 1671176 | tf_op jit(solution)/shard_map/ppermute | solution.py:522
  61.2 8.3 %collective-permute-start.19 = (f32[34,8,128]{2,1,0:T(8,128)S(1)}, f32[34,8,128]{2,1,0:T(8,128)S(1)}, u32[]{:S(2)}, u32[]{:S(2)}) collective-permute-start(f32[34,8,128]{2,1,0:T(8,128)S(1)} %copy-done.15), channel_id=1, source_target_pairs={{0,16},{1,17},{8,24},{9,25},{16,0},{17,1},{24,8},{25,9},{2,18},{3,... | collective-permute-start | bytes 417800 | tf_op jit(solution)/shard_map/ppermute | solution.py:498
  61.5 12.2 %collective-permute-start.20 = (f32[34,8,128]{2,1,0:T(8,128)S(1)}, f32[34,8,128]{2,1,0:T(8,128)S(1)}, u32[]{:S(2)}, u32[]{:S(2)}) collective-permute-start(f32[34,8,128]{2,1,0:T(8,128)S(1)} %copy-done.14), channel_id=1, source_target_pairs={{0,17},{1,16},{8,25},{9,24},{16,1},{17,0},{24,9},{25,8},{2,19},{3,... | collective-permute-start | bytes 417800 | tf_op jit(solution)/shard_map/ppermute | solution.py:498
  64.3 10.8 %collective-permute-start.21 = (f32[34,8,128]{2,1,0:T(8,128)S(1)}, f32[34,8,128]{2,1,0:T(8,128)S(1)}, u32[]{:S(2)}, u32[]{:S(2)}) collective-permute-start(f32[34,8,128]{2,1,0:T(8,128)S(1)} %copy-done.13), channel_id=1, source_target_pairs={{0,24},{1,25},{8,16},{9,17},{16,8},{17,9},{24,0},{25,1},{2,26},{3,... | collective-permute-start | bytes 417800 | tf_op jit(solution)/shard_map/ppermute | solution.py:498
  69.5 31.4 %collective-permute-start.8 = (f32[4,32,4,128]{3,2,1,0:T(4,128)S(1)}, f32[4,32,4,128]{3,2,1,0:T(4,128)S(1)}, u32[]{:S(2)}, u32[]{:S(2)}) collective-permute-start(f32[4,32,4,128]{3,2,1,0:T(4,128)S(1)} %pad_maximum_fusion.3), channel_id=1, source_target_pairs={{0,2},{2,4},{3,1},{4,6},{5,3},{7,5},{8,10},{10,12},{11,9},{12,14},... | collective-permute-start | bytes 786440 | tf_op jit(solution)/shard_map/ppermute | solution.py:522
  73.7 27.3 %collective-permute-start.3 = (f32[4,32,4,128]{3,2,1,0:T(4,128)S(1)}, f32[4,32,4,128]{3,2,1,0:T(4,128)S(1)}, u32[]{:S(2)}, u32[]{:S(2)}) collective-permute-start(f32[4,32,4,128]{3,2,1,0:T(4,128)S(1)} %pad_maximum_fusion.2), channel_id=1, source_target_pairs={{1,3},{2,0},{3,5},{4,2},{5,7},{6,4},{9,11},{10,8},{11,13},{12,10},... | collective-permute-start | bytes 786440 | tf_op jit(solution)/shard_map/ppermute | solution.py:522
  75.0 7.1 %collective-permute-start.22 = (f32[34,8,128]{2,1,0:T(8,128)S(1)}, f32[34,8,128]{2,1,0:T(8,128)S(1)}, u32[]{:S(2)}, u32[]{:S(2)}) collective-permute-start(f32[34,8,128]{2,1,0:T(8,128)S(1)} %copy-done.12), channel_id=1, source_target_pairs={{0,25},{1,24},{8,17},{9,16},{16,9},{17,8},{24,1},{25,0},{2,27},{3,... | collective-permute-start | bytes 417800 | tf_op jit(solution)/shard_map/ppermute | solution.py:498
  104.0 4.5 %collective-permute-start.25 = (f32[4,16,128]{2,1,0:T(8,128)S(1)}, f32[4,16,128]{2,1,0:T(8,128)S(1)}, u32[]{:S(2)}, u32[]{:S(2)}) collective-permute-start(f32[4,16,128]{2,1,0:T(8,128)S(1)} %get-tuple-element.65), channel_id=1, source_target_pairs={{0,1},{1,0},{2,3},{3,2},{4,5},{5,4},{6,7},{7,6},{8,9},{9,8},{10,11... | collective-permute-start | bytes 98312 | tf_op jit(solution)/shard_map/ppermute | solution.py:640
  (16 other events, 678.8 us)
